TPU v7x, 32 devices: a whole 2x2x4 slice. The times are simulated.
32 devices in a mesh: depth: 2 (over core), seq: 16 (over z, y, x).
Axes of the slice: x: 2, y: 2, z: 4, core: 2. Of those that a mesh axis runs over, the one named last changes fastest.
Arguments:
- queries: bfloat16 [2, 2048, 4096], P('depth', 'seq'), may hold values from -27 to 27
- grad_out: bfloat16 [2, 2048, 4096], P('depth', 'seq'), may hold values from -48 to 48
- key_states: bfloat16 [2048, 4096], P('depth', 'seq'), may hold values from -3 to 3
- value_states: bfloat16 [2048, 4096], P('depth', 'seq'), may hold values from -6 to 6
- offsets: int32 [2], replicated, may hold values from 0 to 8, as said below
- windows: int32 [2], replicated, may hold values from 512 to 1024, as said below
Outputs:
- grad_queries: bfloat16 [2, 2048, 4096], P('depth', 'seq')
- grad_keys: bfloat16 [2048, 4096], P('depth', 'seq')
- grad_values: bfloat16 [2048, 4096], P('depth', 'seq')
Inputs may be any that keep to these rules, and one draw needn't show every extreme that they name: `windows`: one depth's window is exactly 1024. `offsets`: one depth's offset is exactly 8.
All inputs are finite; a program needn't handle non-finite values.
Results may differ from a plain program's by a relative error of at most 0.033.
Values may be sent and summed in bfloat16 or wider, within the bound.
No kernel may reach another device: no remote copies, remote signals or barrier semaphores. Data moves between devices by JAX's collectives and lax.ppermute only.
A program may use at most 64 MiB of HBM per device.

v0:
```python
import math

import jax
import jax.numpy as jnp
from jax import lax
from jax.sharding import PartitionSpec as P

HEAD_DIM = 128
WIN = 1024
OFF_MAX = 8


def allowed_mask(query_pos, key_pos, shift_now, span_now, seq_total):
    query_col = query_pos[:, None]
    key_row = key_pos[None, :]
    inside = (key_row >= 0) & (key_row < seq_total) & (query_col >= 0) & (query_col < seq_total)
    return (
        inside & (key_row <= query_col + shift_now) & (key_row > query_col + shift_now - span_now)
    )


def head_scores(query_blk, key_blk):
    scaling = 1.0 / math.sqrt(HEAD_DIM)
    return (
        jnp.einsum("qhd,khd->hqk", query_blk, key_blk, preferred_element_type=jnp.float32) * scaling
    )


def on_device(queries, grad_out, key_states, value_states, offsets, windows):
    scaling = 1.0 / math.sqrt(HEAD_DIM)
    depth_id = lax.axis_index("depth")
    picked = jnp.arange(offsets.shape[0], dtype=jnp.int32) == depth_id
    shift_now = jnp.sum(jnp.where(picked, offsets, 0))
    span_now = jnp.sum(jnp.where(picked, windows, 0))
    tok_rows = queries.shape[1]
    model_width = queries.shape[2]
    query_heads, grad_heads = (
        lax.all_to_all(
            queries.reshape(tok_rows, model_width), "seq", split_axis=1, concat_axis=0, tiled=True
        ),
        lax.all_to_all(
            grad_out.reshape(tok_rows, model_width), "seq", split_axis=1, concat_axis=0, tiled=True
        ),
    )
    key_all, value_all = (
        lax.all_gather(key_states, "depth", axis=0, tiled=True),
        lax.all_gather(value_states, "depth", axis=0, tiled=True),
    )
    seq_total = query_heads.shape[0]
    width = query_heads.shape[1]
    head_count = width // HEAD_DIM
    depth_rows = seq_total // lax.axis_size("depth")
    block_len = min(512, depth_rows)
    blocks = seq_total // block_len
    span_keys = block_len + WIN
    query3 = query_heads.reshape(seq_total, head_count, HEAD_DIM)
    grad3 = grad_heads.reshape(seq_total, head_count, HEAD_DIM)
    key3 = key_all.reshape(seq_total, head_count, HEAD_DIM)
    value3 = value_all.reshape(seq_total, head_count, HEAD_DIM)
    widths = ((WIN, OFF_MAX + 1), (0, 0), (0, 0))
    key_pad = jnp.pad(key3, widths)
    value_pad = jnp.pad(value3, widths)

    def block_grads(number):
        first_row = number * block_len
        key_first = first_row + shift_now + 1
        query_blk = lax.dynamic_slice_in_dim(query3, first_row, block_len, 0)
        grad_blk = lax.dynamic_slice_in_dim(grad3, first_row, block_len, 0)
        key_blk = lax.dynamic_slice_in_dim(key_pad, key_first, span_keys, 0)
        value_blk = lax.dynamic_slice_in_dim(value_pad, key_first, span_keys, 0)
        scores = head_scores(query_blk, key_blk)
        query_pos = first_row + jnp.arange(block_len, dtype=jnp.int32)
        key_pos = key_first - WIN + jnp.arange(span_keys, dtype=jnp.int32)
        allowed = allowed_mask(query_pos, key_pos, shift_now, span_now, seq_total)
        masked = jnp.where(allowed[None], scores, -jnp.inf)
        highest = jnp.max(masked, axis=2, keepdims=True)
        log_total = highest + jnp.log(jnp.sum(jnp.exp(masked - highest), axis=2, keepdims=True))
        probs = jnp.exp(masked - log_total)
        weights = probs.astype(jnp.bfloat16)
        grad_probs = jnp.einsum(
            "qhd,khd->hqk", grad_blk, value_blk, preferred_element_type=jnp.float32
        )
        row_dot = jnp.sum(weights.astype(jnp.float32) * grad_probs, axis=2, keepdims=True)
        grad_scores = (probs * (grad_probs - row_dot)).astype(jnp.bfloat16)
        grad_query = (
            jnp.einsum("hqk,khd->qhd", grad_scores, key_blk, preferred_element_type=jnp.float32)
            * scaling
        )
        return (
            grad_query,
            grad_scores,
            weights,
            query_blk,
            grad_blk,
            key_first,
            log_total[:, :, 0],
            row_dot[:, :, 0],
        )

    def query_only(number):
        outcome = block_grads(number)
        return (outcome[0], outcome[6], outcome[7])

    grad_rows, totals, row_dots = lax.map(query_only, jnp.arange(blocks, dtype=jnp.int32))
    query_pad = jnp.pad(query3, ((OFF_MAX, WIN), (0, 0), (0, 0)))
    grad_pad = jnp.pad(grad3, ((OFF_MAX, WIN), (0, 0), (0, 0)))
    total_flat = jnp.transpose(totals, (1, 0, 2)).reshape(head_count, seq_total)
    dot_flat = jnp.transpose(row_dots, (1, 0, 2)).reshape(head_count, seq_total)
    total_pad = jnp.pad(total_flat, ((0, 0), (OFF_MAX, WIN)))
    dot_pad = jnp.pad(dot_flat, ((0, 0), (OFF_MAX, WIN)))

    def one_block(piece_id):
        key_first = piece_id * block_len
        key_blk = lax.dynamic_slice_in_dim(key3, key_first, block_len, 0)
        value_blk = lax.dynamic_slice_in_dim(value3, key_first, block_len, 0)
        query_first = key_first - shift_now + OFF_MAX
        query_blk = lax.dynamic_slice_in_dim(query_pad, query_first, span_keys, 0)
        grad_blk = lax.dynamic_slice_in_dim(grad_pad, query_first, span_keys, 0)
        log_total = lax.dynamic_slice_in_dim(total_pad, query_first, span_keys, 1)
        row_dot = lax.dynamic_slice_in_dim(dot_pad, query_first, span_keys, 1)
        scores = head_scores(query_blk, key_blk)
        query_pos = key_first - shift_now + jnp.arange(span_keys, dtype=jnp.int32)
        key_pos = key_first + jnp.arange(block_len, dtype=jnp.int32)
        allowed = allowed_mask(query_pos, key_pos, shift_now, span_now, seq_total)
        probs = jnp.exp(jnp.where(allowed[None], scores - log_total[:, :, None], -jnp.inf))
        weights = probs.astype(jnp.bfloat16)
        grad_probs = jnp.einsum(
            "qhd,khd->hqk", grad_blk, value_blk, preferred_element_type=jnp.float32
        )
        grad_scores = (probs * (grad_probs - row_dot[:, :, None])).astype(jnp.bfloat16)
        key_term = (
            jnp.einsum("hqk,qhd->khd", grad_scores, query_blk, preferred_element_type=jnp.float32)
            * scaling
        )
        value_term = jnp.einsum(
            "hqk,qhd->khd", weights, grad_blk, preferred_element_type=jnp.float32
        )
        return jnp.concatenate(
            [key_term.reshape(block_len, width), value_term.reshape(block_len, width)], axis=1
        )

    pieces = lax.map(
        one_block, jnp.arange(depth_rows * lax.axis_size("depth") // block_len, dtype=jnp.int32)
    )
    summed = lax.psum_scatter(
        pieces.reshape(depth_rows * lax.axis_size("depth"), 2 * width).astype(jnp.bfloat16),
        "depth",
        scatter_dimension=0,
        tiled=True,
    ).astype(jnp.float32)
    grad_query = grad_rows.reshape(seq_total, width).astype(jnp.bfloat16)
    grad_back = lax.all_to_all(grad_query, "seq", split_axis=0, concat_axis=1, tiled=True)
    grad_keys = summed[:, :width].astype(jnp.bfloat16)
    grad_values = summed[:, width:].astype(jnp.bfloat16)
    return (grad_back.reshape(1, tok_rows, model_width), grad_keys, grad_values)


def solution(mesh):
    in_specs = (
        P("depth", "seq", None),
        P("depth", "seq", None),
        P("depth", "seq"),
        P("depth", "seq"),
        P(),
        P(),
    )
    out_specs = (P("depth", "seq", None), P("depth", "seq"), P("depth", "seq"))
    return jax.shard_map(
        on_device, mesh=mesh, in_specs=in_specs, out_specs=out_specs, check_vma=False
    )
```

profile of v0, /device:TPU:0, one launch (start us, length us, event | category | flops | bytes accessed | tf_op | source)
XLA Modules:
  0.0 275.9 jit_solution(11988162052669328171)
XLA Ops:
  7.2 2.4 copy.64
  9.6 8.3 %all-to-all-start = ((bf16[128,16,256]{0,2,1:T(8,128)(2,1)}), bf16[128,16,256]{0,2,1:T(8,128)(2,1)S(1)}, u32[]{:S(2)}, u32[]{:S(2)}) async-start(bf16[128,16,256]{0,2,1:T(8,128)(2,1)} %bitcast.12), calls=%async_computation | async-start | bytes 2097152 | tf_op jit(solution)/shard_map/all_to_all | solution.py:38
  18.0 2.0 copy.63
  20.1 1.3 copy.66
  21.4 20.9 %all-to-all-done = bf16[128,16,256]{0,2,1:T(8,128)(2,1)S(1)} async-done(((bf16[128,16,256]{0,2,1:T(8,128)(2,1)}), bf16[128,16,256]{0,2,1:T(8,128)(2,1)S(1)}, u32[]{:S(2)}, u32[]{:S(2)}) %all-to-all-start) | async-done | bytes 1048608 | tf_op jit(solution)/shard_map/all_to_all | solution.py:38
  42.3 5.9 %all-to-all-start.1 = ((bf16[128,16,256]{0,2,1:T(8,128)(2,1)}), bf16[128,16,256]{0,2,1:T(8,128)(2,1)}, u32[]{:S(2)}, u32[]{:S(2)}) async-start(bf16[128,16,256]{0,2,1:T(8,128)(2,1)} %bitcast.14), calls=%async_computation.1 | async-start | bytes 2097152 | tf_op jit(solution)/shard_map/all_to_all | solution.py:41
  50.2 1.3 pad.21
  51.5 10.0 %all-gather.5.cloned.1.call-done = bf16[2048,256]{0,1:T(8,128)(2,1)} async-done(((bf16[1024,256]{0,1:T(8,128)(2,1)}), bf16[2048,256]{0,1:T(8,128)(2,1)}) %all-gather.5.cloned.1.call-update) | async-done | bytes 1048592 | tf_op jit(solution)/shard_map/all_gather | solution.py:47
  61.5 2.5 pad.22
  64.0 1.7 copy.65
  65.7 2.3 reshape.374
  68.0 3.3 %all-to-all-done.1 = bf16[128,16,256]{0,2,1:T(8,128)(2,1)} async-done(((bf16[128,16,256]{0,2,1:T(8,128)(2,1)}), bf16[128,16,256]{0,2,1:T(8,128)(2,1)}, u32[]{:S(2)}, u32[]{:S(2)}) %all-to-all-start.1) | async-done | bytes 1048608 | tf_op jit(solution)/shard_map/all_to_all | solution.py:41
  71.3 2.9 %copy.67 = bf16[16,128,256]{1,0,2:T(8,128)(2,1)} copy(bf16[16,128,256]{1,2,0:T(8,128)(2,1)} %bitcast.15) | data formatting | bytes 2097152 | tf_op jit(solution)/shard_map/all_to_all | solution.py:41
  74.2 1.5 reshape.375
  75.7 2.9 %pad.23 = bf16[3080,2,128]{0,2,1:T(8,128)(2,1)} pad(bf16[2048,2,128]{0,2,1:T(8,128)(2,1)} %reshape.374, bf16[]{:T(256)} %constant.156.clone.1), padding=8_1024x0_0x0_0 | pad | bytes 2625538 | tf_op jit(solution)/shard_map/jit(_pad)/pad | solution.py:105
  78.6 1.6 pad.25
  80.2 58.7 %while.30 = (s32[]{:T(128)}, bf16[4,512,2,128]{1,3,2,0:T(8,128)(2,1)}, f32[4,2,512]{2,1,0:T(2,128)S(1)}, f32[4,2,512]{2,1,0:T(2,128)S(1)}, s32[4]{0:T(128)S(1)},...) while((s32[]{:T(128)}, ...), condition=%wide.region_6.7_spmd, body=%wide.region_2.6_spmd.sunk | while | flops 1234838016 | bytes 51197324 | solution.py:104
  82.1 1.3 fusion.67
  83.4 1.4 compare_and_fusion.9
  84.9 2.8 fusion.69
  87.6 1.0 exponential_reduce_fusion.2
  88.7 3.0 %multiply_reduce_fusion.2 = (f32[2,512]{1,0:T(2,128)S(1)}, f32[2,512,1536]{2,1,0:T(8,128)S(1)}) fusion(f32[2,512,1536]{2,1,0:T(8,128)S(1)} %get-tuple-element.679, f32[2,512]{1,0:T(2,128)S(1)} %get-tuple-element.681, bf16[3081,2,128]{0,2,1:T(8,128)(2,1)} %get-tuple-element.746, s32[]{:T(128)S(6)} %select_n.85, ...), kind=kOutput, calls=%fused_computation.1.clone.1 | convolution fusion | flops 410516480 | bytes 13639688 | tf_op jit(solution)/shard_map/while/body/eval_jaxpr/qhd,khd->hqk/dot_general | solution.py:80
  91.7 2.2 fusion.70
  96.8 1.3 fusion.67
  98.1 1.4 compare_and_fusion.9
  99.5 2.8 %fusion.69 = (f32[2,512]{1,0:T(2,128)S(1)}, f32[2,512,1536]{2,1,0:T(8,128)S(1)}) fusion(bf16[3081,2,128]{0,2,1:T(8,128)(2,1)S(1)} %get-tuple-element.742, s32[]{:T(128)S(6)} %select_n.85, bf16[2048,2,128]{0,2,1:T(8,128)(2,1)} %get-tuple-element.744, s32[]{:T(128)S(6)} %select_n.86, pred[512,1536]{1,0:T(8,128)(4,1)S(1)} %compare_and_fusion.9), kind=kOutput, calls=%fused_computation.67.clone.1 | convolution fusion | flops 407370752 | bytes 8130568 | tf_op jit(solution)/shard_map/while/body/eval_jaxpr/qhd,khd->hqk/dot_general | solution.py:25
  102.3 1.0 exponential_reduce_fusion.2
  103.4 3.0 %multiply_reduce_fusion.2 = (f32[2,512]{1,0:T(2,128)S(1)}, f32[2,512,1536]{2,1,0:T(8,128)S(1)}) fusion(f32[2,512,1536]{2,1,0:T(8,128)S(1)} %get-tuple-element.679, f32[2,512]{1,0:T(2,128)S(1)} %get-tuple-element.681, bf16[3081,2,128]{0,2,1:T(8,128)(2,1)} %get-tuple-element.746, s32[]{:T(128)S(6)} %select_n.85, ...), kind=kOutput, calls=%fused_computation.1.clone.1 | convolution fusion | flops 410516480 | bytes 13639688 | tf_op jit(solution)/shard_map/while/body/eval_jaxpr/qhd,khd->hqk/dot_general | solution.py:80
  106.4 2.2 fusion.70
  111.5 1.3 fusion.67
  112.8 1.4 compare_and_fusion.9
  114.2 2.8 fusion.69
  118.0 3.0 %multiply_reduce_fusion.2 = (f32[2,512]{1,0:T(2,128)S(1)}, f32[2,512,1536]{2,1,0:T(8,128)S(1)}) fusion(f32[2,512,1536]{2,1,0:T(8,128)S(1)} %get-tuple-element.679, f32[2,512]{1,0:T(2,128)S(1)} %get-tuple-element.681, bf16[3081,2,128]{0,2,1:T(8,128)(2,1)} %get-tuple-element.746, s32[]{:T(128)S(6)} %select_n.85, ...), kind=kOutput, calls=%fused_computation.1.clone.1 | convolution fusion | flops 410516480 | bytes 13639688 | tf_op jit(solution)/shard_map/while/body/eval_jaxpr/qhd,khd->hqk/dot_general | solution.py:80
  121.1 2.2 fusion.70
  126.1 1.3 fusion.67
  127.5 1.4 compare_and_fusion.9
  128.9 2.8 fusion.69
  132.7 3.0 %multiply_reduce_fusion.2 = (f32[2,512]{1,0:T(2,128)S(1)}, f32[2,512,1536]{2,1,0:T(8,128)S(1)}) fusion(f32[2,512,1536]{2,1,0:T(8,128)S(1)} %get-tuple-element.679, f32[2,512]{1,0:T(2,128)S(1)} %get-tuple-element.681, bf16[3081,2,128]{0,2,1:T(8,128)(2,1)} %get-tuple-element.746, s32[]{:T(128)S(6)} %select_n.85, ...), kind=kOutput, calls=%fused_computation.1.clone.1 | convolution fusion | flops 410516480 | bytes 13639688 | tf_op jit(solution)/shard_map/while/body/eval_jaxpr/qhd,khd->hqk/dot_general | solution.py:80
  135.8 2.2 fusion.70
  139.1 89.5 %while.31 = (s32[]{:T(128)}, bf16[4,512,512]{1,2,0:T(8,128)(2,1)}, s32[4]{0:T(128)S(1)}, s32[]{:T(128)}, bf16[3080,2,128]{0,2,1:T(8,128)(2,1)}, /*index=5*/s32[]...) while((s32[]{:T(128)}, bf16[4,512,512]{1,2,0:T(8,128)(2,1)}, ...), condition=%wide.region_8.9_spmd, body=%wide.region_7.8_spmd.sunk | while | flops 1632382464 | bytes 32908628 | solution.py:142
  141.2 5.4 %fusion.78 = f32[2,1536,512]{2,1,0:T(8,128)} fusion(bf16[3080,2,128]{0,2,1:T(8,128)(2,1)} %get-tuple-element.791, s32[]{:T(128)S(6)} %select_n.89, bf16[2048,2,128]{0,2,1:T(8,128)(2,1)} %get-tuple-element.793, s32[]{:T(128)S(6)} %select_n.90), kind=kOutput, calls=%fused_computation.42.clone.1 | convolution fusion | flops 402653184 | bytes 7340040 | tf_op jit(solution)/shard_map/while/body/eval_jaxpr/qhd,khd->hqk/dot_general | solution.py:25
  146.6 1.3 fusion.79
  148.0 1.8 compare_and_fusion.11
  149.9 6.7 %fusion.82 = bf16[2,128,512]{2,1,0:T(8,128)(2,1)S(1)} fusion(f32[2,1536,512]{2,1,0:T(8,128)} %fusion.78, f32[2,1536]{1,0:T(2,128)S(1)} %get-tuple-element.701, f32[2,1536]{1,0:T(2,128)S(1)} %get-tuple-element.696, pred[1536,512]{1,0:T(8,128)(4,1)S(1)} %compare_and_fusion.11, bf16[3080,2,128]{0,2,1:T(8,128)(2,1)S(1)} %copy-done, s32[]{:T(128)S(6)} %select_n.89, ...), kind=kOutput, calls=%fused_computation.37.clone.1 | convolution fusion | flops 815005696 | bytes 9201152 | tf_op jit(solution)/shard_map/while/body/eval_jaxpr/hqk,qhd->khd/dot_general | solution.py:132
  156.5 4.3 %fusion.81 = bf16[2,128,512]{2,1,0:T(8,128)(2,1)S(1)} fusion(f32[2,1536,512]{2,1,0:T(8,128)} %fusion.78, f32[2,1536]{1,0:T(2,128)S(1)} %get-tuple-element.696, pred[1536,512]{1,0:T(8,128)(4,1)S(1)} %compare_and_fusion.11, bf16[3080,2,128]{0,2,1:T(8,128)(2,1)S(1)} %copy-done, s32[]{:T(128)S(6)} %select_n.89), kind=kOutput, calls=%fused_computation.33.clone.1 | convolution fusion | flops 408944640 | bytes 8138756 | tf_op jit(solution)/shard_map/while/body/eval_jaxpr/hqk,qhd->khd/dot_general | solution.py:135
  163.5 5.4 %fusion.78 = f32[2,1536,512]{2,1,0:T(8,128)} fusion(bf16[3080,2,128]{0,2,1:T(8,128)(2,1)} %get-tuple-element.791, s32[]{:T(128)S(6)} %select_n.89, bf16[2048,2,128]{0,2,1:T(8,128)(2,1)} %get-tuple-element.793, s32[]{:T(128)S(6)} %select_n.90), kind=kOutput, calls=%fused_computation.42.clone.1 | convolution fusion | flops 402653184 | bytes 7340040 | tf_op jit(solution)/shard_map/while/body/eval_jaxpr/qhd,khd->hqk/dot_general | solution.py:25
  168.9 1.3 fusion.79
  170.3 1.8 compare_and_fusion.11
  172.2 6.7 %fusion.82 = bf16[2,128,512]{2,1,0:T(8,128)(2,1)S(1)} fusion(f32[2,1536,512]{2,1,0:T(8,128)} %fusion.78, f32[2,1536]{1,0:T(2,128)S(1)} %get-tuple-element.701, f32[2,1536]{1,0:T(2,128)S(1)} %get-tuple-element.696, pred[1536,512]{1,0:T(8,128)(4,1)S(1)} %compare_and_fusion.11, bf16[3080,2,128]{0,2,1:T(8,128)(2,1)S(1)} %copy-done, s32[]{:T(128)S(6)} %select_n.89, ...), kind=kOutput, calls=%fused_computation.37.clone.1 | convolution fusion | flops 815005696 | bytes 9201152 | tf_op jit(solution)/shard_map/while/body/eval_jaxpr/hqk,qhd->khd/dot_general | solution.py:132
  178.8 4.3 %fusion.81 = bf16[2,128,512]{2,1,0:T(8,128)(2,1)S(1)} fusion(f32[2,1536,512]{2,1,0:T(8,128)} %fusion.78, f32[2,1536]{1,0:T(2,128)S(1)} %get-tuple-element.696, pred[1536,512]{1,0:T(8,128)(4,1)S(1)} %compare_and_fusion.11, bf16[3080,2,128]{0,2,1:T(8,128)(2,1)S(1)} %copy-done, s32[]{:T(128)S(6)} %select_n.89), kind=kOutput, calls=%fused_computation.33.clone.1 | convolution fusion | flops 408944640 | bytes 8138756 | tf_op jit(solution)/shard_map/while/body/eval_jaxpr/hqk,qhd->khd/dot_general | solution.py:135
  185.8 5.4 %fusion.78 = f32[2,1536,512]{2,1,0:T(8,128)} fusion(bf16[3080,2,128]{0,2,1:T(8,128)(2,1)} %get-tuple-element.791, s32[]{:T(128)S(6)} %select_n.89, bf16[2048,2,128]{0,2,1:T(8,128)(2,1)} %get-tuple-element.793, s32[]{:T(128)S(6)} %select_n.90), kind=kOutput, calls=%fused_computation.42.clone.1 | convolution fusion | flops 402653184 | bytes 7340040 | tf_op jit(solution)/shard_map/while/body/eval_jaxpr/qhd,khd->hqk/dot_general | solution.py:25
  191.2 1.3 fusion.79
  192.6 1.8 compare_and_fusion.11
  194.5 6.7 %fusion.82 = bf16[2,128,512]{2,1,0:T(8,128)(2,1)S(1)} fusion(f32[2,1536,512]{2,1,0:T(8,128)} %fusion.78, f32[2,1536]{1,0:T(2,128)S(1)} %get-tuple-element.701, f32[2,1536]{1,0:T(2,128)S(1)} %get-tuple-element.696, pred[1536,512]{1,0:T(8,128)(4,1)S(1)} %compare_and_fusion.11, bf16[3080,2,128]{0,2,1:T(8,128)(2,1)S(1)} %copy-done, s32[]{:T(128)S(6)} %select_n.89, ...), kind=kOutput, calls=%fused_computation.37.clone.1 | convolution fusion | flops 815005696 | bytes 9201152 | tf_op jit(solution)/shard_map/while/body/eval_jaxpr/hqk,qhd->khd/dot_general | solution.py:132
  201.1 4.3 %fusion.81 = bf16[2,128,512]{2,1,0:T(8,128)(2,1)S(1)} fusion(f32[2,1536,512]{2,1,0:T(8,128)} %fusion.78, f32[2,1536]{1,0:T(2,128)S(1)} %get-tuple-element.696, pred[1536,512]{1,0:T(8,128)(4,1)S(1)} %compare_and_fusion.11, bf16[3080,2,128]{0,2,1:T(8,128)(2,1)S(1)} %copy-done, s32[]{:T(128)S(6)} %select_n.89), kind=kOutput, calls=%fused_computation.33.clone.1 | convolution fusion | flops 408944640 | bytes 8138756 | tf_op jit(solution)/shard_map/while/body/eval_jaxpr/hqk,qhd->khd/dot_general | solution.py:135
  208.1 5.4 %fusion.78 = f32[2,1536,512]{2,1,0:T(8,128)} fusion(bf16[3080,2,128]{0,2,1:T(8,128)(2,1)} %get-tuple-element.791, s32[]{:T(128)S(6)} %select_n.89, bf16[2048,2,128]{0,2,1:T(8,128)(2,1)} %get-tuple-element.793, s32[]{:T(128)S(6)} %select_n.90), kind=kOutput, calls=%fused_computation.42.clone.1 | convolution fusion | flops 402653184 | bytes 7340040 | tf_op jit(solution)/shard_map/while/body/eval_jaxpr/qhd,khd->hqk/dot_general | solution.py:25
  213.5 1.3 fusion.79
  214.9 1.8 compare_and_fusion.11
  216.8 6.7 %fusion.82 = bf16[2,128,512]{2,1,0:T(8,128)(2,1)S(1)} fusion(f32[2,1536,512]{2,1,0:T(8,128)} %fusion.78, f32[2,1536]{1,0:T(2,128)S(1)} %get-tuple-element.701, f32[2,1536]{1,0:T(2,128)S(1)} %get-tuple-element.696, pred[1536,512]{1,0:T(8,128)(4,1)S(1)} %compare_and_fusion.11, bf16[3080,2,128]{0,2,1:T(8,128)(2,1)S(1)} %copy-done, s32[]{:T(128)S(6)} %select_n.89, ...), kind=kOutput, calls=%fused_computation.37.clone.1 | convolution fusion | flops 815005696 | bytes 9201152 | tf_op jit(solution)/shard_map/while/body/eval_jaxpr/hqk,qhd->khd/dot_general | solution.py:132
  223.4 4.3 %fusion.81 = bf16[2,128,512]{2,1,0:T(8,128)(2,1)S(1)} fusion(f32[2,1536,512]{2,1,0:T(8,128)} %fusion.78, f32[2,1536]{1,0:T(2,128)S(1)} %get-tuple-element.696, pred[1536,512]{1,0:T(8,128)(4,1)S(1)} %compare_and_fusion.11, bf16[3080,2,128]{0,2,1:T(8,128)(2,1)S(1)} %copy-done, s32[]{:T(128)S(6)} %select_n.89), kind=kOutput, calls=%fused_computation.33.clone.1 | convolution fusion | flops 408944640 | bytes 8138756 | tf_op jit(solution)/shard_map/while/body/eval_jaxpr/hqk,qhd->khd/dot_general | solution.py:135
  228.6 4.2 %copy.79 = bf16[4,512,512]{2,1,0:T(8,128)(2,1)} copy(bf16[4,512,512]{1,2,0:T(8,128)(2,1)} %get-tuple-element.363) | data formatting | bytes 4194304 | tf_op jit(solution)/shard_map/convert_element_type | solution.py:146
  234.4 30.7 %all_to_all.45 = bf16[16,128,256]{2,1,0:T(8,128)(2,1)S(1)} all-to-all(bf16[16,128,256]{2,1,0:T(8,128)(2,1)S(1)} %convert_element_type.65), channel_id=1, replica_groups=mesh['depth'=2,'seq'=16] {'seq'}, dimensions={0} | all-to-all | bytes 2097152 | tf_op jit(solution)/shard_map/all_to_all | solution.py:152
  265.8 1.3 copy.80
  267.1 2.2 fusion.47
  (105 shorter events, 18.9 us)
Async XLA Ops:
  7.2 12.9 %copy-start.1 = (bf16[1,128,4096]{2,1,0:T(8,128)(2,1)S(1)}, bf16[1,128,4096]{2,1,0:T(8,128)(2,1)}, u32[]{:S(2)}) copy-start(bf16[1,128,4096]{2,1,0:T(8,128)(2,1)} %param.11) | copy-start | bytes 3145732
  7.2 41.1 %copy-start.5 = (bf16[1024,256]{1,0:T(8,128)(2,1)S(1)}, bf16[1024,256]{1,0:T(8,128)(2,1)}, u32[]{:S(2)}) copy-start(bf16[1024,256]{1,0:T(8,128)(2,1)} %param.13) | copy-start | bytes 1572868
  7.2 42.3 %copy-start.6 = (s32[2]{0:T(128)S(1)}, s32[2]{0:T(128)}, u32[]{:S(2)}) copy-start(s32[2]{0:T(128)} %param.14) | copy-start | bytes 28
  7.2 42.3 %copy-start.7 = (s32[2]{0:T(128)S(1)}, s32[2]{0:T(128)}, u32[]{:S(2)}) copy-start(s32[2]{0:T(128)} %param.15) | copy-start | bytes 28
  9.6 32.7 %all-to-all-start = ((bf16[128,16,256]{0,2,1:T(8,128)(2,1)}), bf16[128,16,256]{0,2,1:T(8,128)(2,1)S(1)}, u32[]{:S(2)}, u32[]{:S(2)}) async-start(bf16[128,16,256]{0,2,1:T(8,128)(2,1)} %bitcast.12), calls=%async_computation | async-start | bytes 2097152 | tf_op jit(solution)/shard_map/all_to_all | solution.py:38
  17.9 32.2 %all-gather.3.cloned.1.call-start = ((), (), s32[]{:S(2)}) async-start(), calls=%async_computation.4 | async-start | bytes 1572864 | tf_op jit(solution)/shard_map/all_gather | solution.py:46
  42.3 29.0 %all-to-all-start.1 = ((bf16[128,16,256]{0,2,1:T(8,128)(2,1)}), bf16[128,16,256]{0,2,1:T(8,128)(2,1)}, u32[]{:S(2)}, u32[]{:S(2)}) async-start(bf16[128,16,256]{0,2,1:T(8,128)(2,1)} %bitcast.14), calls=%async_computation.1 | async-start | bytes 2097152 | tf_op jit(solution)/shard_map/all_to_all | solution.py:41
  48.3 13.2 %all-gather.5.cloned.1.call-start = ((), (), s32[]{:S(2)}) async-start(), calls=%async_computation.5 | async-start | bytes 1572864 | tf_op jit(solution)/shard_map/all_gather | solution.py:47
  49.3 217.8 %reduce-scatter.2.cloned.1.call-start = ((), (), s32[]{:S(2)}) async-start(), calls=%async_computation.6 | async-start | bytes 3145728 | tf_op jit(solution)/shard_map/reduce_scatter | solution.py:145
  88.7 3.1 %copy-start.2 = (bf16[4,512,2,128]{1,3,2,0:T(8,128)(2,1)S(1)}, bf16[4,512,2,128]{1,3,2,0:T(8,128)(2,1)}, u32[]{:S(2)}) copy-start(bf16[4,512,2,128]{1,3,2,0:T(8,128)(2,1)} %get-tuple-element.720) | copy-start | bytes 3145732 | tf_op jit(solution)/shard_map/while
  93.9 1.0 copy-start.3
  103.4 3.1 %copy-start.2 = (bf16[4,512,2,128]{1,3,2,0:T(8,128)(2,1)S(1)}, bf16[4,512,2,128]{1,3,2,0:T(8,128)(2,1)}, u32[]{:S(2)}) copy-start(bf16[4,512,2,128]{1,3,2,0:T(8,128)(2,1)} %get-tuple-element.720) | copy-start | bytes 3145732 | tf_op jit(solution)/shard_map/while
  108.6 1.0 copy-start.3
  118.0 3.1 %copy-start.2 = (bf16[4,512,2,128]{1,3,2,0:T(8,128)(2,1)S(1)}, bf16[4,512,2,128]{1,3,2,0:T(8,128)(2,1)}, u32[]{:S(2)}) copy-start(bf16[4,512,2,128]{1,3,2,0:T(8,128)(2,1)} %get-tuple-element.720) | copy-start | bytes 3145732 | tf_op jit(solution)/shard_map/while
  123.3 1.0 copy-start.3
  132.7 3.1 %copy-start.2 = (bf16[4,512,2,128]{1,3,2,0:T(8,128)(2,1)S(1)}, bf16[4,512,2,128]{1,3,2,0:T(8,128)(2,1)}, u32[]{:S(2)}) copy-start(bf16[4,512,2,128]{1,3,2,0:T(8,128)(2,1)} %get-tuple-element.720) | copy-start | bytes 3145732 | tf_op jit(solution)/shard_map/while
  138.0 1.0 copy-start.3
  139.3 10.5 %copy-start = (bf16[3080,2,128]{0,2,1:T(8,128)(2,1)S(1)}, bf16[3080,2,128]{0,2,1:T(8,128)(2,1)}, u32[]{:S(2)}) copy-start(bf16[3080,2,128]{0,2,1:T(8,128)(2,1)} %get-tuple-element.795) | copy-start | bytes 4730884 | tf_op jit(solution)/shard_map/while
  161.6 10.5 %copy-start = (bf16[3080,2,128]{0,2,1:T(8,128)(2,1)S(1)}, bf16[3080,2,128]{0,2,1:T(8,128)(2,1)}, u32[]{:S(2)}) copy-start(bf16[3080,2,128]{0,2,1:T(8,128)(2,1)} %get-tuple-element.795) | copy-start | bytes 4730884 | tf_op jit(solution)/shard_map/while
  184.0 10.5 %copy-start = (bf16[3080,2,128]{0,2,1:T(8,128)(2,1)S(1)}, bf16[3080,2,128]{0,2,1:T(8,128)(2,1)}, u32[]{:S(2)}) copy-start(bf16[3080,2,128]{0,2,1:T(8,128)(2,1)} %get-tuple-element.795) | copy-start | bytes 4730884 | tf_op jit(solution)/shard_map/while
  206.2 10.5 %copy-start = (bf16[3080,2,128]{0,2,1:T(8,128)(2,1)S(1)}, bf16[3080,2,128]{0,2,1:T(8,128)(2,1)}, u32[]{:S(2)}) copy-start(bf16[3080,2,128]{0,2,1:T(8,128)(2,1)} %get-tuple-element.795) | copy-start | bytes 4730884 | tf_op jit(solution)/shard_map/while
  228.6 4.3 %copy-start.4 = (bf16[4,512,2,128]{1,3,2,0:T(8,128)(2,1)S(1)}, bf16[4,512,2,128]{1,3,2,0:T(8,128)(2,1)}, u32[]{:S(2)}) copy-start(bf16[4,512,2,128]{1,3,2,0:T(8,128)(2,1)} %get-tuple-element.360) | copy-start | bytes 3145732
Sparse Core Ops, SparseCore 0:
  20.9 10.3 all-gather.2
  51.2 10.2 all-gather.4
  233.0 10.1 reduce-scatter.1
where the time goes:
time: 277 us; the launch traced here: 276 us
  matrix products  97.2 us (35%)
  local copies, waits for them, and re-layouts  42.6 us (15%)
  waiting for transfers between devices  34.3 us (12%)
  other arithmetic  31.7 us (11%)
  blocking collectives  30.7 us (11%)
  starting transfers between devices  14.4 us (5%)
  between operations  13.9 us (5%)
  loops' own time  11 us (4%)
    dot_general x8, matrix products, head_scores(): jnp.einsum('qhd,khd->hqk', query_blk, key_blk, preferred_element_type=jnp...  32.6 us
    all_to_all x1, blocking collectives, on_device(): lax.all_to_all(grad_query, 'seq', split_axis=0, concat_axis=1, tiled=True)  30.7 us
    dot_general x4, matrix products, one_block(): jnp.einsum('hqk,qhd->khd', grad_scores, query_blk, preferred_element_type...  26.7 us
    all_to_all x1, waiting for transfers between devices, on_device(): lax.all_to_all(queries.reshape(tok_rows, model_width), 'seq', split_axis=...  20.9 us
    dot_general x4, matrix products, one_block(): jnp.einsum('hqk,qhd->khd', weights, grad_blk, preferred_element_type=jnp....  17.1 us
    and x8, other arithmetic, allowed_mask(): inside & (key_row <= query_col + shift_now)  12.8 us
    dot_general x4, matrix products, block_grads(): jnp.einsum('qhd,khd->hqk', grad_blk, value_blk, preferred_element_type=jn...  12.2 us
    add x8, other arithmetic, allowed_mask(): query_col + shift_now  10.5 us
  transfers between devices with their start and end apart: 5, of which 3 were waited for; matrix products, arithmetic and copies ran while one was open for 6% of the time, Pallas kernels for 0%

commit v1 on v0

v1 whole, which is shorter than its diff:
```python
import functools
import math

import jax
import jax.numpy as jnp
from jax import lax
from jax.experimental import pallas as pl
from jax.experimental.pallas import tpu as pltpu
from jax.sharding import PartitionSpec as P

HEAD_DIM = 128
WIN = 1024
WIN_MIN = 512
OFF_MAX = 8
EDGE = 16
SCALING = 1.0 / math.sqrt(HEAD_DIM)
EXP2_SCALE = SCALING * math.log2(math.e)


def nt_dot(a, b):
    return lax.dot_general(a, b, (((1,), (1,)), ((), ())), preferred_element_type=jnp.float32)


def nn_dot(a, b):
    return lax.dot_general(a, b, (((1,), (0,)), ((), ())), preferred_element_type=jnp.float32)


def backward_kernel(
    block, past, n_blocks,
    spans_ref, q_ref, g_ref, k_ref, v_ref,
    dq_ref, dk_ref, dv_ref,
    kt_ref, s_ref, p_ref, dk_acc, dv_acc,
):
    number = pl.program_id(1)
    shift = spans_ref[0]
    span = spans_ref[1]
    seq_total = n_blocks * block

    @pl.when(number == 0)
    def _():
        kt_ref[...] = k_ref[...].T
        dk_acc[...] = jnp.zeros_like(dk_acc)
        dv_acc[...] = jnp.zeros_like(dv_acc)

    def step(n_past):
        first_row = pl.multiple_of(number * block, block)
        query = q_ref[...]
        grad = g_ref[...]
        tiles = [
            (pl.multiple_of((number - back) * block, block), block, (n_past - back) * block, -back * block)
            for back in range(n_past, -1, -1)
        ]
        edge_first = pl.multiple_of(
            jnp.minimum(first_row + block, seq_total - EDGE), EDGE
        )
        edge_row = (n_past + 1) * block
        highest = jnp.full((1, block), -jnp.inf, jnp.float32)
        steps_off = lax.broadcasted_iota(jnp.int32, (block, block), 0) - lax.broadcasted_iota(
            jnp.int32, (block, block), 1
        )
        for key_first, rows, at, lead in tiles:
            score = nt_dot(k_ref[pl.ds(key_first, rows), :], query)
            if lead + block - 1 > 0:
                score = jnp.where(steps_off <= shift - lead, score, -jnp.inf)
            if lead - block + 1 <= OFF_MAX - WIN_MIN:
                score = jnp.where(steps_off > shift - span - lead, score, -jnp.inf)
            s_ref[pl.ds(at, rows), :] = score
            highest = jnp.maximum(highest, jnp.max(score, axis=0, keepdims=True))
        edge_score = nt_dot(k_ref[pl.ds(edge_first, EDGE), :], query)
        edge_key = edge_first + lax.broadcasted_iota(jnp.int32, (EDGE, block), 0)
        edge_query = first_row + lax.broadcasted_iota(jnp.int32, (EDGE, block), 1)
        edge_in = (edge_key >= first_row + block) & (edge_key - edge_query <= shift)
        edge_score = jnp.where(edge_in, edge_score, -jnp.inf)
        s_ref[pl.ds(edge_row, EDGE), :] = edge_score
        highest = jnp.maximum(highest, jnp.max(edge_score, axis=0, keepdims=True))

        tiles.append((edge_first, EDGE, edge_row, None))
        total = jnp.zeros((1, block), jnp.float32)
        dotted = jnp.zeros((1, block), jnp.float32)
        for key_first, rows, at, _ in tiles:
            part = jnp.exp2((s_ref[pl.ds(at, rows), :] - highest) * EXP2_SCALE)
            grad_prob = nt_dot(v_ref[pl.ds(key_first, rows), :], grad)
            s_ref[pl.ds(at, rows), :] = part
            p_ref[pl.ds(at, rows), :] = grad_prob
            total = total + jnp.sum(part, axis=0, keepdims=True)
            dotted = dotted + jnp.sum(part * grad_prob, axis=0, keepdims=True)
        inverse = 1.0 / total
        row_dot = dotted * inverse

        dq_t = jnp.zeros((HEAD_DIM, block), jnp.float32)
        for key_first, rows, at, _ in tiles:
            prob = s_ref[pl.ds(at, rows), :] * inverse
            weight = prob.astype(jnp.bfloat16)
            grad_score = (prob * (p_ref[pl.ds(at, rows), :] - row_dot)).astype(jnp.bfloat16)
            here = pl.ds(key_first, rows)
            dv_acc[here, :] += nn_dot(weight, grad)
            dk_acc[here, :] += nn_dot(grad_score, query)
            if rows == EDGE:
                dq_t = dq_t + lax.dot_general(
                    k_ref[here, :], grad_score, (((0,), (0,)), ((), ())),
                    preferred_element_type=jnp.float32,
                )
            else:
                dq_t = dq_t + nn_dot(kt_ref[:, here], grad_score)
        dq_ref[...] = (dq_t * SCALING).T.astype(jnp.bfloat16)

    for n_past in range(past):
        pl.when(number == n_past)(functools.partial(step, n_past))
    pl.when(number >= past)(functools.partial(step, past))

    @pl.when(number == n_blocks - 1)
    def _():
        dk_ref[...] = (dk_acc[...] * SCALING).astype(jnp.bfloat16)
        dv_ref[...] = dv_acc[...].astype(jnp.bfloat16)


def attention_backward(spans, query, grad, key, value):
    seq_total, width = query.shape
    heads = width // HEAD_DIM
    block = min(256, seq_total)
    n_blocks = seq_total // block
    past = min(WIN // block, n_blocks - 1)
    rows = (past + 1) * block + EDGE
    row_spec = pl.BlockSpec((block, HEAD_DIM), lambda h, i, _: (i, h))
    head_spec = pl.BlockSpec((seq_total, HEAD_DIM), lambda h, i, _: (0, h))
    whole = jax.ShapeDtypeStruct((seq_total, width), jnp.bfloat16)
    pairs = heads * seq_total * rows
    return pl.pallas_call(
        functools.partial(backward_kernel, block, past, n_blocks),
        grid_spec=pltpu.PrefetchScalarGridSpec(
            num_scalar_prefetch=1,
            grid=(heads, n_blocks),
            in_specs=[row_spec, row_spec, head_spec, head_spec],
            out_specs=[row_spec, head_spec, head_spec],
            scratch_shapes=[
                pltpu.VMEM((HEAD_DIM, seq_total), jnp.bfloat16),
                pltpu.VMEM((rows, block), jnp.float32),
                pltpu.VMEM((rows, block), jnp.float32),
                pltpu.VMEM((seq_total, HEAD_DIM), jnp.float32),
                pltpu.VMEM((seq_total, HEAD_DIM), jnp.float32),
            ],
        ),
        out_shape=[whole, whole, whole],
        cost_estimate=pl.CostEstimate(
            flops=10 * pairs * HEAD_DIM, bytes_accessed=14 * seq_total * width, transcendentals=pairs
        ),
        name="attention_backward",
    )(spans, query, grad, key, value)


def on_device(queries, grad_out, key_states, value_states, offsets, windows):
    depth_id = lax.axis_index("depth")
    depths = lax.axis_size("depth")
    seq_parts = lax.axis_size("seq")
    spans = jnp.stack([offsets[depth_id], windows[depth_id]])
    tok_rows = queries.shape[1]
    model_width = queries.shape[2]
    width = model_width // seq_parts
    seq_total = tok_rows * seq_parts
    key_rows = key_states.shape[0]

    both = jnp.concatenate([queries, grad_out], axis=0)
    both = jnp.transpose(both.reshape(2, tok_rows, seq_parts, width), (2, 0, 1, 3))
    both = lax.all_to_all(both, "seq", split_axis=0, concat_axis=0, tiled=True)
    query = both[:, 0].reshape(seq_total, width)
    grad = both[:, 1].reshape(seq_total, width)

    if depths == 2:
        swap = [(0, 1), (1, 0)]
        first = depth_id == 0

        def gather(mine):
            other = lax.ppermute(mine, "depth", swap)
            return jnp.concatenate(
                [jnp.where(first, mine, other), jnp.where(first, other, mine)], axis=0
            )

        def scatter(part):
            mine = lax.dynamic_slice_in_dim(part, depth_id * key_rows, key_rows, 0)
            given = lax.dynamic_slice_in_dim(part, (1 - depth_id) * key_rows, key_rows, 0)
            other = lax.ppermute(given, "depth", swap)
            return (mine.astype(jnp.float32) + other.astype(jnp.float32)).astype(jnp.bfloat16)
    else:

        def gather(mine):
            return lax.all_gather(mine, "depth", axis=0, tiled=True)

        def scatter(part):
            return lax.psum_scatter(part, "depth", scatter_dimension=0, tiled=True)

    key_all = gather(key_states)
    value_all = gather(value_states)
    dq, dk, dv = attention_backward(spans, query, grad, key_all, value_all)
    grad_keys = scatter(dk)
    grad_values = scatter(dv)
    back = lax.all_to_all(
        dq.reshape(seq_parts, tok_rows, width), "seq", split_axis=0, concat_axis=0, tiled=True
    )
    back = jnp.transpose(back, (1, 0, 2)).reshape(1, tok_rows, model_width)
    return back, grad_keys, grad_values


def solution(mesh):
    in_specs = (
        P("depth", "seq", None),
        P("depth", "seq", None),
        P("depth", "seq"),
        P("depth", "seq"),
        P(),
        P(),
    )
    out_specs = (P("depth", "seq", None), P("depth", "seq"), P("depth", "seq"))
    return jax.shard_map(
        on_device, mesh=mesh, in_specs=in_specs, out_specs=out_specs, check_vma=False
    )
```

time: 277 us -> 121 us (0.44)
  matrix products: 97.2 us -> 0 us
  local copies, waits for them, and re-layouts: 42.6 us -> 11.9 us
  blocking collectives: 30.7 us -> 0 us
  Pallas kernels: 0 us -> 23.4 us
  other arithmetic: 31.7 us -> 10.7 us
  waiting for transfers between devices: 34.3 us -> 53.4 us
  between operations: 13.9 us -> 0.74 us
  loops' own time: 11 us -> 0 us
  starting transfers between devices: 14.4 us -> 19.7 us
    dot_general x24 -> x0, matrix products: 97.2 us -> none  [the longest x8 32.6 us: head_scores(): jnp.einsum('qhd,khd->hqk', query_blk, key_blk, preferred_element_type=jnp...]
    all_to_all x1 -> x0, blocking collectives: 30.7 us -> none  [on_device(): lax.all_to_all(grad_query, 'seq', split_axis=0, concat_axis=1, tiled=True)]
    all_to_all x2, waiting for transfers between devices: 24.2 us -> 52.5 us  [the longest x1 35.9 us: on_device(): both = lax.all_to_all(both, 'seq', split_axis=0, concat_axis=0, tiled=True)]
    pallas_call x0 -> x1, Pallas kernels: none -> 23.4 us  [attention_backward(): pl.pallas_call(functools.partial(backward_kernel, block, past, n_blocks),...]
    and x16 -> x0, other arithmetic: 12.8 us -> none  [the longest x8 12.8 us: allowed_mask(): inside & (key_row <= query_col + shift_now)]
    another operation x2 -> x0, loops' own time: 11 us -> none  [the longest x1 5.59 us: on_device(): lax.map(one_block, jnp.arange(depth_rows * lax.axis_size('depth') // bloc...]
    add x16 -> x0, other arithmetic: 10.5 us -> none  [the longest x8 10.5 us: allowed_mask(): query_col + shift_now]
    all_gather x2 -> x0, waiting for transfers between devices: 9.97 us -> none  [the longest x1 9.97 us: on_device(): lax.all_gather(value_states, 'depth', axis=0, tiled=True)]
  transfers between devices with their start and end apart: 5 -> 6, of which waited for: 3 -> 3; matrix products, arithmetic and copies ran while one was open for 6% -> 10% of each run, Pallas kernels for 0% -> 0%
where the time goes in v1:
time: 121 us; the launch traced here: 120 us
  waiting for transfers between devices  53.4 us (44%)
  Pallas kernels  23.4 us (19%)
  starting transfers between devices  19.7 us (16%)
  local copies, waits for them, and re-layouts  11.9 us (10%)
  other arithmetic  10.7 us (9%)
    all_to_all x1, waiting for transfers between devices, on_device(): both = lax.all_to_all(both, 'seq', split_axis=0, concat_axis=0, tiled=True)  35.9 us
    pallas_call x1, Pallas kernels, attention_backward(): pl.pallas_call(functools.partial(backward_kernel, block, past, n_blocks),...  23.4 us
    all_to_all x1, waiting for transfers between devices, on_device(): lax.all_to_all(dq.reshape(seq_parts, tok_rows, width), 'seq', split_axis=...  16.6 us
    all_to_all x1, starting transfers between devices, on_device(): lax.all_to_all(dq.reshape(seq_parts, tok_rows, width), 'seq', split_axis=...  10.2 us
    all_to_all x1, starting transfers between devices, on_device(): both = lax.all_to_all(both, 'seq', split_axis=0, concat_axis=0, tiled=True)  8.48 us
    convert_element_type x2, other arithmetic, scatter(): (mine.astype(jnp.float32) + other.astype(jnp.float32)).astype(jnp.bfloat16)  3.93 us
    unnamed x16, local copies, waits for them, and re-layouts  3.04 us
    transpose x1, local copies, waits for them, and re-layouts, on_device(): jnp.transpose(both.reshape(2, tok_rows, seq_parts, width), (2, 0, 1, 3))  2.64 us
  transfers between devices with their start and end apart: 6, of which 3 were waited for; matrix products, arithmetic and copies ran while one was open for 10% of the time, Pallas kernels for 0%

profile of v1, /device:TPU:0, one launch (start us, length us, event | category | flops | bytes accessed | tf_op | source)
XLA Modules:
  0.0 119.8 jit_solution(11117769085292972810)
XLA Ops:
  0.6 0.0 copy-start
  0.6 1.7 %copy.12 = bf16[1,128,4096]{1,2,0:T(8,128)(2,1)S(1)} copy(bf16[1,128,4096]{2,1,0:T(8,128)(2,1)} %param.6) | data formatting | bytes 2097152 | tf_op args[0]
  2.4 0.0 copy-done
  2.4 1.3 %copy.13 = bf16[1,128,4096]{1,2,0:T(8,128)(2,1)} copy(bf16[1,128,4096]{2,1,0:T(8,128)(2,1)S(1)} %copy-done) | data formatting | bytes 2097152 | tf_op args[1]
  3.7 1.4 %pad_maximum_fusion = bf16[2,128,4096]{1,2,0:T(8,128)(2,1)S(1)} fusion(bf16[1,128,4096]{1,2,0:T(8,128)(2,1)} %copy.13, bf16[1,128,4096]{1,2,0:T(8,128)(2,1)S(1)} %copy.12), kind=kLoop, calls=%fused_computation | loop fusion | flops 1048576 | bytes 4194304 | tf_op jit(solution)/shard_map/concatenate | solution.py:162
  5.1 2.6 %copy.14 = bf16[16,2,128,256]{3,2,1,0:T(8,128)(2,1)} copy(bf16[16,2,128,256]{2,3,0,1:T(8,128)(2,1)S(1)} %bitcast.7) | data formatting | bytes 4194304 | tf_op jit(solution)/shard_map/transpose | solution.py:163
  7.7 0.0 copy-start.4
  7.7 0.0 copy-start.3
  7.7 0.0 copy-start.5
  7.7 0.0 copy-start.6
  7.7 8.5 %all-to-all-start = ((bf16[16,2,128,256]{3,2,1,0:T(8,128)(2,1)}), bf16[16,2,128,256]{3,2,1,0:T(8,128)(2,1)S(1)}, u32[]{:S(2)}, u32[]{:S(2)}) async-start(bf16[16,2,128,256]{3,2,1,0:T(8,128)(2,1)} %copy.14), calls=%async_computation | async-start | bytes 4194304 | tf_op jit(solution)/shard_map/all_to_all | solution.py:164
  16.2 0.0 copy-done.4
  16.2 0.1 collective-permute-start
  16.3 0.0 copy-done.3
  16.3 0.5 collective-permute-start.1
  16.8 0.0 copy-done.5
  16.8 0.6 dynamic_slice.18
  17.4 0.0 copy-done.6
  17.4 0.6 dynamic_slice.19
  18.0 1.9 %pad_add_fusion.spans_ref = s32[2]{0:T(128)} fusion(s32[1]{0:T(128)} %dynamic_slice.19, s32[1]{0:T(128)} %dynamic_slice.18), kind=kLoop, calls=%fused_computation.11 | loop fusion | flops 2 | bytes 16 | tf_op jit(solution)/shard_map/stack | solution.py:155
  19.9 0.0 collective-permute-done
  19.9 0.0 collective-permute-done.1
  19.9 1.3 %broadcast_select_fusion.1 = (bf16[1024,256]{1,0:T(8,128)(2,1)S(1)}, bf16[1024,256]{1,0:T(8,128)(2,1)S(1)}, bf16[1024,256]{1,0:T(8,128)(2,1)S(1)}, bf16[1024,256]{1,0:T(8,128)(2,1)S(1)}) fusion(bf16[1024,256]{1,0:T(8,128)(2,1)S(1)} %copy-done.3, bf16[1024,256]{1,0:T(8,128)(2,1)} %collective-permute-done.1, pred[]{:T(512)S(6)} %eq.3, ...), kind=kLoop, calls=%fused_computation.6 | loop fusion | flops 1048576 | bytes 4194305 | tf_op jit(solution)/shard_map/jit(_where)/select_n | solution.py:175
  21.2 1.0 pad_maximum_fusion.1.k_ref
  22.3 1.1 pad_maximum_fusion.2.v_ref
  23.3 35.9 %all-to-all-done = bf16[16,2,128,256]{3,2,1,0:T(8,128)(2,1)S(1)} async-done(((bf16[16,2,128,256]{3,2,1,0:T(8,128)(2,1)}), bf16[16,2,128,256]{3,2,1,0:T(8,128)(2,1)S(1)}, u32[]{:S(2)}, u32[]{:S(2)}) %all-to-all-start) | async-done | bytes 2097184 | tf_op jit(solution)/shard_map/all_to_all | solution.py:164
  59.3 1.5 %fusion = (bf16[16,1,128,256]{3,2,1,0:T(8,128)(2,1)}, bf16[16,1,128,256]{3,2,1,0:T(8,128)(2,1)}) fusion(bf16[16,2,128,256]{3,2,1,0:T(8,128)(2,1)S(1)} %all-to-all-done), kind=kLoop, calls=%fused_computation.12 | loop fusion | bytes 4194304 | tf_op jit(solution)/shard_map/slice | solution.py:166
  60.7 23.4 %attention_backward.1 = (bf16[2048,256]{1,0:T(8,128)(2,1)}, bf16[2048,256]{1,0:T(8,128)(2,1)}, bf16[2048,256]{1,0:T(8,128)(2,1)}) custom-call(s32[2]{0:T(128)} %pad_add_fusion.spans_ref, bf16[2048,256]{1,0:T(8,128)(2,1)} %bitcast.11, bf16[2048,256]{1,0:T(8,128)(2,1)} %bitcast.10, bf16[2048,256]{1,0:T(8,128)(2,1)} %pad_maximum_fusion.1.k_ref, ...), custom_call_target="tpu_custom_call" | custom-call | flops 6794772480 | bytes 7340032 | tf_op jit(solution)/shard_map/attention_backward/pallas_call | solution.py:128
  84.2 0.0 copy-start.2
  84.2 0.0 copy-start.1
  84.2 10.2 %all-to-all-start.1 = ((bf16[16,128,256]{2,1,0:T(8,128)(2,1)}), bf16[16,128,256]{2,1,0:T(8,128)(2,1)S(1)}, u32[]{:S(2)}, u32[]{:S(2)}) async-start(bf16[16,128,256]{2,1,0:T(8,128)(2,1)} %bitcast.9), calls=%async_computation.1 | async-start | bytes 2097152 | tf_op jit(solution)/shard_map/all_to_all | solution.py:196
  94.3 0.0 copy-done.2
  94.4 0.8 constant_dynamic-slice_fusion
  95.2 0.0 collective-permute-start.3
  95.2 0.0 copy-done.1
  95.2 0.8 constant_dynamic-slice_fusion.1
  96.0 0.5 collective-permute-start.2
  96.5 0.9 collective-permute-done.3
  97.4 2.0 %add_convert_fusion = bf16[1024,256]{1,0:T(8,128)(2,1)} fusion(bf16[1024,256]{1,0:T(8,128)(2,1)} %collective-permute-done.3, bf16[2048,256]{1,0:T(8,128)(2,1)S(1)} %copy-done.2, s32[]{:T(128)S(6)} %select_n.38), kind=kLoop, calls=%fused_computation.3 | loop fusion | flops 1048576 | bytes 1572868 | tf_op jit(solution)/shard_map/convert_element_type | solution.py:182
  99.4 0.0 collective-permute-done.2
  99.4 2.0 %add_convert_fusion.1 = bf16[1024,256]{1,0:T(8,128)(2,1)} fusion(bf16[1024,256]{1,0:T(8,128)(2,1)} %collective-permute-done.2, bf16[2048,256]{1,0:T(8,128)(2,1)S(1)} %copy-done.1, s32[]{:T(128)S(6)} %select_n.38), kind=kLoop, calls=%fused_computation.4 | loop fusion | flops 1048576 | bytes 1572868 | tf_op jit(solution)/shard_map/convert_element_type | solution.py:182
  101.4 16.6 %all-to-all-done.1 = bf16[16,128,256]{2,1,0:T(8,128)(2,1)S(1)} async-done(((bf16[16,128,256]{2,1,0:T(8,128)(2,1)}), bf16[16,128,256]{2,1,0:T(8,128)(2,1)S(1)}, u32[]{:S(2)}, u32[]{:S(2)}) %all-to-all-start.1) | async-done | bytes 1048608 | tf_op jit(solution)/shard_map/all_to_all | solution.py:196
  117.9 0.6 copy.15
  118.5 1.3 %reshape.17 = bf16[1,128,4096]{2,1,0:T(8,128)(2,1)} reshape(bf16[128,16,256]{2,1,0:T(8,128)(2,1)S(1)} %copy.15) | data formatting | bytes 2097152 | tf_op jit(solution)/shard_map/reshape | solution.py:199
Async XLA Ops:
  0.6 1.7 %copy-start = (bf16[1,128,4096]{2,1,0:T(8,128)(2,1)S(1)}, bf16[1,128,4096]{2,1,0:T(8,128)(2,1)}, u32[]{:S(2)}) copy-start(bf16[1,128,4096]{2,1,0:T(8,128)(2,1)} %param.7) | copy-start | bytes 3145732
  7.7 8.5 %copy-start.4 = (bf16[1024,256]{1,0:T(8,128)(2,1)S(1)}, bf16[1024,256]{1,0:T(8,128)(2,1)}, u32[]{:S(2)}) copy-start(bf16[1024,256]{1,0:T(8,128)(2,1)} %param.8) | copy-start | bytes 1572868
  7.7 8.6 %copy-start.3 = (bf16[1024,256]{1,0:T(8,128)(2,1)S(1)}, bf16[1024,256]{1,0:T(8,128)(2,1)}, u32[]{:S(2)}) copy-start(bf16[1024,256]{1,0:T(8,128)(2,1)} %param.9) | copy-start | bytes 1572868
  7.7 9.1 %copy-start.5 = (s32[2]{0:T(128)S(1)}, s32[2]{0:T(128)}, u32[]{:S(2)}) copy-start(s32[2]{0:T(128)} %param.10) | copy-start | bytes 28
  7.7 9.7 %copy-start.6 = (s32[2]{0:T(128)S(1)}, s32[2]{0:T(128)}, u32[]{:S(2)}) copy-start(s32[2]{0:T(128)} %param.11) | copy-start | bytes 28
  7.7 51.5 %all-to-all-start = ((bf16[16,2,128,256]{3,2,1,0:T(8,128)(2,1)}), bf16[16,2,128,256]{3,2,1,0:T(8,128)(2,1)S(1)}, u32[]{:S(2)}, u32[]{:S(2)}) async-start(bf16[16,2,128,256]{3,2,1,0:T(8,128)(2,1)} %copy.14), calls=%async_computation | async-start | bytes 4194304 | tf_op jit(solution)/shard_map/all_to_all | solution.py:164
  16.2 3.6 %collective-permute-start = (bf16[1024,256]{1,0:T(8,128)(2,1)S(1)}, bf16[1024,256]{1,0:T(8,128)(2,1)}, u32[]{:S(2)}, u32[]{:S(2)}) collective-permute-start(bf16[1024,256]{1,0:T(8,128)(2,1)S(1)} %copy-done.4), channel_id=1, source_target_pairs={{0,16},{16,0},{1,17},{17,1},{2,18},{18,2},{3,19},{19,3},{4,20},{20... | collective-permute-start | bytes 1572872 | tf_op jit(solution)/shard_map/ppermute | solution.py:173
  16.3 3.5 %collective-permute-start.1 = (bf16[1024,256]{1,0:T(8,128)(2,1)S(1)}, bf16[1024,256]{1,0:T(8,128)(2,1)}, u32[]{:S(2)}, u32[]{:S(2)}) collective-permute-start(bf16[1024,256]{1,0:T(8,128)(2,1)S(1)} %copy-done.3), channel_id=1, source_target_pairs={{0,16},{16,0},{1,17},{17,1},{2,18},{18,2},{3,19},{19,3},{4,20},{20... | collective-permute-start | bytes 1572872 | tf_op jit(solution)/shard_map/ppermute | solution.py:173
  84.2 10.2 %copy-start.2 = (bf16[2048,256]{1,0:T(8,128)(2,1)S(1)}, bf16[2048,256]{1,0:T(8,128)(2,1)}, u32[]{:S(2)}) copy-start(bf16[2048,256]{1,0:T(8,128)(2,1)} %get-tuple-element.8) | copy-start | bytes 3145732
  84.2 11.0 %copy-start.1 = (bf16[2048,256]{1,0:T(8,128)(2,1)S(1)}, bf16[2048,256]{1,0:T(8,128)(2,1)}, u32[]{:S(2)}) copy-start(bf16[2048,256]{1,0:T(8,128)(2,1)} %get-tuple-element.7) | copy-start | bytes 3145732
  84.2 33.8 %all-to-all-start.1 = ((bf16[16,128,256]{2,1,0:T(8,128)(2,1)}), bf16[16,128,256]{2,1,0:T(8,128)(2,1)S(1)}, u32[]{:S(2)}, u32[]{:S(2)}) async-start(bf16[16,128,256]{2,1,0:T(8,128)(2,1)} %bitcast.9), calls=%async_computation.1 | async-start | bytes 2097152 | tf_op jit(solution)/shard_map/all_to_all | solution.py:196
  95.2 2.3 %collective-permute-start.3 = (bf16[1024,256]{1,0:T(8,128)(2,1)}, bf16[1024,256]{1,0:T(8,128)(2,1)}, u32[]{:S(2)}, u32[]{:S(2)}) collective-permute-start(bf16[1024,256]{1,0:T(8,128)(2,1)} %constant_dynamic-slice_fusion), channel_id=1, source_target_pairs={{0,16},{16,0},{1,17},{17,1},{2,18},{18,2},{3,19},{19,3},{4,20},{20... | collective-permute-start | bytes 1572872 | tf_op jit(solution)/shard_map/ppermute | solution.py:181
  96.0 3.4 %collective-permute-start.2 = (bf16[1024,256]{1,0:T(8,128)(2,1)}, bf16[1024,256]{1,0:T(8,128)(2,1)}, u32[]{:S(2)}, u32[]{:S(2)}) collective-permute-start(bf16[1024,256]{1,0:T(8,128)(2,1)} %constant_dynamic-slice_fusion.1), channel_id=1, source_target_pairs={{0,16},{16,0},{1,17},{17,1},{2,18},{18,2},{3,19},{19,3},{4,20},{20... | collective-permute-start | bytes 1572872 | tf_op jit(solution)/shard_map/ppermute | solution.py:181

commit v2 on v1

v2 whole, which is shorter than its diff:
```python
import functools
import math

import jax
import jax.numpy as jnp
from jax import lax
from jax.experimental import pallas as pl
from jax.experimental.pallas import tpu as pltpu
from jax.sharding import PartitionSpec as P


HEAD_DIM = 128
WIN = 1024
EDGE = 16
SCALING = 1.0 / math.sqrt(HEAD_DIM)
EXP2_SCALE = SCALING * math.log2(math.e)
LOWEST = -1e30


def nt_dot(a, b):
    return lax.dot_general(a, b, (((1,), (1,)), ((), ())), preferred_element_type=jnp.float32)


def nn_dot(a, b):
    return lax.dot_general(a, b, (((1,), (0,)), ((), ())), preferred_element_type=jnp.float32)


def backward_kernel(block, past, n_blocks, n_pieces, n_parts, *refs):
    scalars, *refs = refs
    if n_pieces == 1:
        q_ref, g_ref, *refs = refs
    else:
        pieces, refs = refs[:n_pieces], refs[n_pieces:]
    key_parts, refs = refs[:n_parts], refs[n_parts:]
    value_parts, refs = refs[:n_parts], refs[n_parts:]
    dq_ref, dk_ref, dv_ref, k_ref, v_ref, kt_ref, bias_ref, p_ref, gp_ref, dk_acc, dv_acc, *refs = refs

    number = pl.program_id(0)
    shift = scalars[0]
    span = scalars[1]
    seq_total = n_blocks * block

    @pl.when(number == 0)
    def _():
        part_rows = seq_total // n_parts
        for n in range(n_parts):
            here = pl.ds(pl.multiple_of(scalars[2 + n], part_rows), part_rows)
            k_ref[here, :] = key_parts[n][...]
            v_ref[here, :] = value_parts[n][...]
        kt_ref[...] = k_ref[...].T
        dk_acc[...] = jnp.zeros_like(dk_acc)
        dv_acc[...] = jnp.zeros_like(dv_acc)
        ahead = lax.broadcasted_iota(jnp.int32, (block, block), 0) - lax.broadcasted_iota(
            jnp.int32, (block, block), 1
        )
        for back in range(past + 1):
            here = ahead - back * block
            bias_ref[back] = jnp.where((here <= shift) & (here > shift - span), 0.0, -jnp.inf)
        if n_pieces > 1:
            places = pieces[0].shape[0]
            for n in range(n_pieces):
                refs[0][pl.ds(scalars[2 + n_parts + n], places)] = pieces[n][...]

    def step(n_past):
        first_row = pl.multiple_of(number * block, block)
        if n_pieces == 1:
            query = q_ref[...].reshape(block, HEAD_DIM)
            grad = g_ref[...].reshape(block, HEAD_DIM)
        else:
            rows = pieces[0].shape[2]
            held = refs[0][pl.ds(number * (block // rows), block // rows)]
            query = held[:, 0].reshape(block, HEAD_DIM)
            grad = held[:, 1].reshape(block, HEAD_DIM)
        edge_first = pl.multiple_of(jnp.minimum(first_row + block, seq_total - EDGE), EDGE)
        edge_key = edge_first + lax.broadcasted_iota(jnp.int32, (EDGE, block), 0)
        edge_query = first_row + lax.broadcasted_iota(jnp.int32, (EDGE, block), 1)
        edge_in = (edge_key >= first_row + block) & (edge_key - edge_query <= shift)
        tiles = [
            (pl.multiple_of((number - back) * block, block), block, back * block, back)
            for back in range(n_past + 1)
        ]
        tiles.append((edge_first, EDGE, (past + 1) * block, None))

        highest = jnp.full((1, block), LOWEST, jnp.float32)
        total = jnp.zeros((1, block), jnp.float32)
        dotted = jnp.zeros((1, block), jnp.float32)
        highs = []
        for key_first, rows, at, back in tiles:
            score = nt_dot(k_ref[pl.ds(key_first, rows), :], query)
            if back is None:
                score = jnp.where(edge_in, score, -jnp.inf)
            else:
                score = score + bias_ref[back]
            now = jnp.maximum(highest, jnp.max(score, axis=0, keepdims=True))
            part = jnp.exp2((score - now) * EXP2_SCALE)
            grad_prob = nt_dot(v_ref[pl.ds(key_first, rows), :], grad)
            p_ref[pl.ds(at, rows), :] = part
            gp_ref[pl.ds(at, rows), :] = grad_prob
            less = jnp.exp2((highest - now) * EXP2_SCALE)
            total = total * less + jnp.sum(part, axis=0, keepdims=True)
            dotted = dotted * less + jnp.sum(part * grad_prob, axis=0, keepdims=True)
            highest = now
            highs.append(now)
        inverse = 1.0 / total
        row_dot = dotted * inverse

        dq_t = jnp.zeros((HEAD_DIM, block), jnp.float32)
        for (key_first, rows, at, back), high in zip(tiles, highs, strict=True):
            prob = p_ref[pl.ds(at, rows), :] * (inverse * jnp.exp2((high - highest) * EXP2_SCALE))
            weight = prob.astype(jnp.bfloat16)
            grad_score = (prob * (gp_ref[pl.ds(at, rows), :] - row_dot)).astype(jnp.bfloat16)
            here = pl.ds(key_first, rows)
            dv_acc[here, :] += nn_dot(weight, grad)
            dk_acc[here, :] += nn_dot(grad_score, query)
            if back is None:
                dq_t = dq_t + lax.dot_general(
                    k_ref[here, :], grad_score, (((0,), (0,)), ((), ())),
                    preferred_element_type=jnp.float32,
                )
            else:
                dq_t = dq_t + nn_dot(kt_ref[:, here], grad_score)
        dq_ref[...] = (dq_t * SCALING).T.astype(jnp.bfloat16).reshape(dq_ref.shape)

    for n_past in range(past):
        pl.when(number == n_past)(functools.partial(step, n_past))
    pl.when(number >= past)(functools.partial(step, past))

    @pl.when(number == n_blocks - 1)
    def _():
        dk_ref[...] = (dk_acc[...] * SCALING).astype(jnp.bfloat16)
        dv_ref[...] = dv_acc[...].astype(jnp.bfloat16)


def attention_backward(scalars, pieces, key_parts, value_parts, head):
    n_pieces, n_parts = len(pieces), len(key_parts)
    places, _, tok_rows, _ = pieces[0].shape
    sources = places * n_pieces
    seq_total = sources * tok_rows
    block = min(2 * tok_rows, seq_total)
    per_block = block // tok_rows
    n_blocks = seq_total // block
    past = min(-(-WIN // block), n_blocks - 1)
    rows = (past + 1) * block + EDGE

    def whole(shape):
        return pl.BlockSpec(shape, lambda i, _: (0,) * len(shape))

    if n_pieces == 1:
        piece_args = [pieces[0], pieces[0]]
        piece_specs = [
            pl.BlockSpec((per_block, 1, tok_rows, HEAD_DIM), lambda i, _, w=which: (i, w, 0, 0))
            for which in range(2)
        ]
        piece_scratch = []
    else:
        piece_args = list(pieces)
        piece_specs = [whole(p.shape) for p in pieces]
        piece_scratch = [pltpu.VMEM((sources, 2, tok_rows, HEAD_DIM), jnp.bfloat16)]
    part_spec = pl.BlockSpec((seq_total // n_parts, HEAD_DIM), lambda i, _: (0, head))
    pairs = seq_total * rows
    f32, bf16 = jnp.float32, jnp.bfloat16
    return pl.pallas_call(
        functools.partial(backward_kernel, block, past, n_blocks, n_pieces, n_parts),
        grid_spec=pltpu.PrefetchScalarGridSpec(
            num_scalar_prefetch=1,
            grid=(n_blocks,),
            in_specs=piece_specs + [part_spec] * (2 * n_parts),
            out_specs=[
                pl.BlockSpec((per_block, tok_rows, HEAD_DIM), lambda i, _: (i, 0, 0)),
                whole((seq_total, HEAD_DIM)),
                whole((seq_total, HEAD_DIM)),
            ],
            scratch_shapes=[
                pltpu.VMEM((seq_total, HEAD_DIM), bf16),
                pltpu.VMEM((seq_total, HEAD_DIM), bf16),
                pltpu.VMEM((HEAD_DIM, seq_total), bf16),
                pltpu.VMEM((past + 1, block, block), f32),
                pltpu.VMEM((rows, block), f32),
                pltpu.VMEM((rows, block), f32),
                pltpu.VMEM((seq_total, HEAD_DIM), f32),
                pltpu.VMEM((seq_total, HEAD_DIM), f32),
            ]
            + piece_scratch,
        ),
        out_shape=[
            jax.ShapeDtypeStruct((sources, tok_rows, HEAD_DIM), bf16),
            jax.ShapeDtypeStruct((seq_total, HEAD_DIM), bf16),
            jax.ShapeDtypeStruct((seq_total, HEAD_DIM), bf16),
        ],
        cost_estimate=pl.CostEstimate(
            flops=10 * pairs * HEAD_DIM, bytes_accessed=14 * seq_total * HEAD_DIM, transcendentals=pairs
        ),
    )(scalars, *piece_args, *key_parts, *value_parts)


def moved(arrays, out_shapes, moves_of, scalars=None):
    n_in = len(arrays)

    def kernel(scalars_ref, *refs):
        ins, outs, sem = refs[:n_in], refs[n_in:-1], refs[-1]
        copies = [
            pltpu.make_async_copy(ins[a].at[source], outs[o].at[target], sem.at[n])
            for n, (a, source, o, target) in enumerate(moves_of(scalars_ref))
        ]
        for copy in copies:
            copy.start()
        for copy in copies:
            copy.wait()

    if scalars is None:
        scalars = jnp.zeros((1,), jnp.int32)
    count = len(moves_of(range(64)))
    return pl.pallas_call(
        kernel,
        in_specs=[pl.BlockSpec(memory_space=pltpu.SMEM)] + [pl.BlockSpec(memory_space=pl.ANY)] * n_in,
        out_specs=[pl.BlockSpec(memory_space=pltpu.VMEM)] * len(out_shapes),
        out_shape=[jax.ShapeDtypeStruct(s, jnp.bfloat16) for s in out_shapes],
        scratch_shapes=[pltpu.SemaphoreType.DMA((count,))],
        cost_estimate=pl.CostEstimate(
            flops=0, bytes_accessed=4 * sum(math.prod(s) for s in out_shapes), transcendentals=0
        ),
    )(scalars, *arrays)


def layout_of(parts):
    near = 1 << (parts.bit_length() // 2)
    far = parts // near
    return near, far, far * near == parts and parts & (parts - 1) == 0 and far > 1


def on_device(queries, grad_out, key_states, value_states, offsets, windows):
    depth_id = lax.axis_index("depth")
    seq_id = lax.axis_index("seq")
    depths = lax.axis_size("depth")
    parts = lax.axis_size("seq")
    tok_rows, model_width = queries.shape[1:]
    key_rows, width = key_states.shape
    heads = width // HEAD_DIM
    queries = queries.reshape(tok_rows, model_width)
    grad_out = grad_out.reshape(tok_rows, model_width)
    near, far, two_step = layout_of(parts)
    near_id, far_id = seq_id % near, seq_id // near
    piece = (2, tok_rows, HEAD_DIM)

    def column(dest, head):
        start = (dest * heads + head) * HEAD_DIM
        if not isinstance(start, int):
            start = pl.multiple_of(start, HEAD_DIM)
        return (slice(None), pl.ds(start, HEAD_DIM))

    def ppermute_xor(array, bits):
        return lax.ppermute(array, "seq", [(i, i ^ bits) for i in range(parts)])

    def send_all(head):
        (sent,) = moved(
            [queries, grad_out], [(parts, *piece)],
            lambda _: [(a, column(d, head), 0, (d, a)) for d in range(parts) for a in range(2)],
        )
        return [lax.all_to_all(sent, "seq", split_axis=0, concat_axis=0, tiled=True)]

    def send_near_then_far(head):
        ids = jnp.stack([near_id, far_id]).astype(jnp.int32)
        first = moved(
            [queries, grad_out], [(far, *piece)] * near,
            lambda s: [
                (a, column(f * near + (s[0] ^ j), head), j, (f, a))
                for j in range(near) for f in range(far) for a in range(2)
            ],
            ids,
        )
        first = [first[0]] + [ppermute_xor(first[j], j) for j in range(1, near)]
        second = moved(
            first, [(near, *piece)] * far,
            lambda s: [(j, s[1] ^ m, m, s[0] ^ j) for m in range(far) for j in range(near)],
            ids,
        )
        return [second[0]] + [ppermute_xor(second[m], m * near) for m in range(1, far)]

    received = [
        send_near_then_far(head) if head and two_step else send_all(head) for head in range(heads)
    ]

    if depths == 2:
        swap = [(0, 1), (1, 0)]
        key_parts = [key_states, lax.ppermute(key_states, "depth", swap)]
        value_parts = [value_states, lax.ppermute(value_states, "depth", swap)]
        starts = [depth_id * key_rows, (1 - depth_id) * key_rows]

        def summed(part):
            mine = lax.dynamic_slice_in_dim(part, depth_id * key_rows, key_rows, 0)
            given = lax.dynamic_slice_in_dim(part, (1 - depth_id) * key_rows, key_rows, 0)
            other = lax.ppermute(given, "depth", swap)
            return (mine.astype(jnp.float32) + other.astype(jnp.float32)).astype(jnp.bfloat16)
    else:
        key_parts = [lax.all_gather(key_states, "depth", axis=0, tiled=True)]
        value_parts = [lax.all_gather(value_states, "depth", axis=0, tiled=True)]
        starts = [0]

        def summed(part):
            return lax.psum_scatter(part, "depth", scatter_dimension=0, tiled=True)

    back, grad_keys, grad_values = [], [], []
    for head in range(heads):
        pieces = received[head]
        places = [0] if len(pieces) == 1 else [(far_id ^ m) * near for m in range(far)]
        scalars = jnp.stack(
            [jnp.asarray(v, jnp.int32) for v in (offsets[depth_id], windows[depth_id], *starts, *places)]
        )
        dq, dk, dv = attention_backward(scalars, pieces, key_parts, value_parts, head)
        back.append(lax.all_to_all(dq, "seq", split_axis=0, concat_axis=0, tiled=True))
        grad_keys.append(summed(dk))
        grad_values.append(summed(dv))

    (grad_queries,) = moved(
        back, [(tok_rows, model_width)],
        lambda _: [(h, d, 0, column(d, h)) for h in range(heads) for d in range(parts)],
    )
    return (
        grad_queries.reshape(1, tok_rows, model_width),
        jnp.concatenate(grad_keys, axis=1),
        jnp.concatenate(grad_values, axis=1),
    )


def solution(mesh):
    in_specs = (
        P("depth", "seq", None),
        P("depth", "seq", None),
        P("depth", "seq"),
        P("depth", "seq"),
        P(),
        P(),
    )
    out_specs = (P("depth", "seq", None), P("depth", "seq"), P("depth", "seq"))
    return jax.shard_map(
        on_device, mesh=mesh, in_specs=in_specs, out_specs=out_specs, check_vma=False
    )
```

time: 121 us -> 132 us (1.091)
  Pallas kernels: 23.4 us -> 37.4 us
  starting transfers between devices: 19.7 us -> 32.4 us
  waiting for transfers between devices: 53.4 us -> 45.9 us
  other arithmetic: 10.7 us -> 3.54 us
    all_to_all x2 -> x3, waiting for transfers between devices: 52.5 us -> 11.9 us  [the longest x2 11.9 us: on_device(): lax.all_to_all(dq, 'seq', split_axis=0, concat_axis=0, tiled=True)]
    ppermute x4 -> x12, waiting for transfers between devices: 0.92 us -> 34 us  [the longest x6 33.6 us: ppermute_xor(): return lax.ppermute(array, 'seq', [(i, i ^ bits) for i in range(parts)])]
    pallas_call x1 -> x6, Pallas kernels: 23.4 us -> 37.4 us  [the longest x2 26.3 us: attention_backward(): pl.pallas_call(functools.partial(backward_kernel, block, past, n_blocks,...]
    ppermute x4 -> x12, starting transfers between devices: 1.07 us -> 9.49 us  [the longest x6 8.03 us: ppermute_xor(): return lax.ppermute(array, 'seq', [(i, i ^ bits) for i in range(parts)])]
    all_to_all x2 -> x3, starting transfers between devices: 18.6 us -> 22.9 us  [the longest x2 14.6 us: on_device(): lax.all_to_all(dq, 'seq', split_axis=0, concat_axis=0, tiled=True)]
    another operation x0 -> x2, local copies, waits for them, and re-layouts: none -> 3.89 us  [on_device(): jnp.stack([jnp.asarray(v, jnp.int32) for v in (offsets[depth_id], windows...]
    transpose x2 -> x0, local copies, waits for them, and re-layouts: 3.23 us -> none  [the longest x1 2.64 us: on_device(): jnp.transpose(both.reshape(2, tok_rows, seq_parts, width), (2, 0, 1, 3))]
    convert_element_type x2 -> x4, other arithmetic: 3.93 us -> 1.24 us  [summed(): (mine.astype(jnp.float32) + other.astype(jnp.float32)).astype(jnp.bfloat16)]
  transfers between devices with their start and end apart: 6 -> 15, of which waited for: 3 -> 7; matrix products, arithmetic and copies ran while one was open for 10% -> 7% of each run, Pallas kernels for 0% -> 25%
where the time goes in v2:
time: 132 us; the launch traced here: 131 us
  waiting for transfers between devices  45.9 us (35%)
  Pallas kernels  37.4 us (28%)
  starting transfers between devices  32.4 us (25%)
  local copies, waits for them, and re-layouts  10.9 us (8%)
  other arithmetic  3.54 us (3%)
    ppermute x6, waiting for transfers between devices, ppermute_xor(): return lax.ppermute(array, 'seq', [(i, i ^ bits) for i in range(parts)])  33.6 us
    pallas_call x2, Pallas kernels, attention_backward(): pl.pallas_call(functools.partial(backward_kernel, block, past, n_blocks,...  26.3 us
    all_to_all x2, starting transfers between devices, on_device(): lax.all_to_all(dq, 'seq', split_axis=0, concat_axis=0, tiled=True)  14.6 us
    all_to_all x2, waiting for transfers between devices, on_device(): lax.all_to_all(dq, 'seq', split_axis=0, concat_axis=0, tiled=True)  11.9 us
    pallas_call x4, Pallas kernels, moved(): pl.pallas_call(kernel, in_specs=[pl.BlockSpec(memory_space=pltpu.SMEM)] +...  11.1 us
    all_to_all x1, starting transfers between devices, send_all(): lax.all_to_all(sent, 'seq', split_axis=0, concat_axis=0, tiled=True)  8.35 us
    ppermute x6, starting transfers between devices, ppermute_xor(): return lax.ppermute(array, 'seq', [(i, i ^ bits) for i in range(parts)])  8.03 us
    unnamed x36, local copies, waits for them, and re-layouts  4.74 us
  transfers between devices with their start and end apart: 15, of which 7 were waited for; matrix products, arithmetic and copies ran while one was open for 7% of the time, Pallas kernels for 25%

profile of v2, /device:TPU:0, one launch (start us, length us, event | category | flops | bytes accessed | tf_op | source)
XLA Modules:
  0.0 131.2 jit_solution(4118290620137834937)
XLA Ops:
  0.6 2.4 %shard_map.85 = bf16[16,2,128,128]{3,2,1,0:T(8,128)(2,1)} custom-call(s32[1]{0:T(128)} %constant.33.clone.1.scalars_ref, bf16[128,4096]{1,0:T(8,128)(2,1)} %bitcast.11, bf16[128,4096]{1,0:T(8,128)(2,1)} %bitcast.13), custom_call_target="tpu_custom_call" | custom-call | bytes 2097152 | tf_op jit(solution)/shard_map/pallas_call | solution.py:213
  3.1 8.4 %all-to-all-start = ((bf16[16,2,128,128]{3,2,1,0:T(8,128)(2,1)}), bf16[16,2,128,128]{3,2,1,0:T(8,128)(2,1)S(1)}, u32[]{:S(2)}, u32[]{:S(2)}) async-start(bf16[16,2,128,128]{3,2,1,0:T(8,128)(2,1)} %shard_map.85), calls=%async_computation | async-start | bytes 2097152 | tf_op jit(solution)/shard_map/all_to_all | solution.py:259
  11.5 0.6 pad_add_fusion.scalars_ref
  12.1 3.2 %shard_map.87 = (bf16[4,2,128,128]{3,2,1,0:T(8,128)(2,1)}, bf16[4,2,128,128]{3,2,1,0:T(8,128)(2,1)}, bf16[4,2,128,128]{3,2,1,0:T(8,128)(2,1)}, bf16[4,2,128,128]{3,2,1,0:T(8,128)(2,1)}) custom-call(s32[2]{0:T(128)} %pad_add_fusion.scalars_ref, bf16[128,4096]{1,0:T(8,128)(2,1)} %bitcast.12, bf16[128,4096]{1,0:T(8,128)(2,1)} %bitcast.14), custom_call_target="tpu_custom_call" | custom-call | bytes 2097152 | tf_op jit(solution)/shard_map/pallas_call | solution.py:213
  15.3 2.0 %collective-permute-start.2 = (bf16[4,2,128,128]{3,2,1,0:T(8,128)(2,1)}, bf16[4,2,128,128]{3,2,1,0:T(8,128)(2,1)S(1)}, u32[]{:S(2)}, u32[]{:S(2)}) collective-permute-start(bf16[4,2,128,128]{3,2,1,0:T(8,128)(2,1)} %get-tuple-element.19), channel_id=1, source_target_pairs={{0,1},{1,0},{2,3},{3,2},{4,5},{5,4},{6,7},{7,6},{8,9},{9,8},{10,11... | collective-permute-start | bytes 786440 | tf_op jit(solution)/shard_map/ppermute | solution.py:252
  17.3 1.5 %collective-permute-start.3 = (bf16[4,2,128,128]{3,2,1,0:T(8,128)(2,1)}, bf16[4,2,128,128]{3,2,1,0:T(8,128)(2,1)S(1)}, u32[]{:S(2)}, u32[]{:S(2)}) collective-permute-start(bf16[4,2,128,128]{3,2,1,0:T(8,128)(2,1)} %get-tuple-element.20), channel_id=1, source_target_pairs={{0,2},{1,3},{2,0},{3,1},{4,6},{5,7},{6,4},{7,5},{8,10},{9,11},{10,... | collective-permute-start | bytes 786440 | tf_op jit(solution)/shard_map/ppermute | solution.py:252
  18.7 0.1 collective-permute-start.4
  18.9 0.0 copy-done.10
  18.9 0.0 collective-permute-start
  18.9 0.0 copy-done.11
  18.9 0.5 collective-permute-start.1
  19.4 11.0 %collective-permute-done.2.refs_1_ = bf16[4,2,128,128]{3,2,1,0:T(8,128)(2,1)S(1)} collective-permute-done((bf16[4,2,128,128]{3,2,1,0:T(8,128)(2,1)}, bf16[4,2,128,128]{3,2,1,0:T(8,128)(2,1)S(1)}, u32[]{:S(2)}, u32[]{:S(2)}) %collective-permute-start.2) | collective-permute-done | bytes 262176 | tf_op jit(solution)/shard_map/ppermute | solution.py:252
  30.4 1.4 %collective-permute-done.3.refs_2_ = bf16[4,2,128,128]{3,2,1,0:T(8,128)(2,1)S(1)} collective-permute-done((bf16[4,2,128,128]{3,2,1,0:T(8,128)(2,1)}, bf16[4,2,128,128]{3,2,1,0:T(8,128)(2,1)S(1)}, u32[]{:S(2)}, u32[]{:S(2)}) %collective-permute-start.3) | collective-permute-done | bytes 262176 | tf_op jit(solution)/shard_map/ppermute | solution.py:252
  31.7 7.3 %collective-permute-done.4.refs_3_ = bf16[4,2,128,128]{3,2,1,0:T(8,128)(2,1)S(1)} collective-permute-done((bf16[4,2,128,128]{3,2,1,0:T(8,128)(2,1)}, bf16[4,2,128,128]{3,2,1,0:T(8,128)(2,1)S(1)}, u32[]{:S(2)}, u32[]{:S(2)}) %collective-permute-start.4) | collective-permute-done | bytes 262176 | tf_op jit(solution)/shard_map/ppermute | solution.py:252
  39.0 0.0 copy-done.7
  39.0 0.7 copy-done.9
  39.7 3.0 %shard_map.88 = (bf16[4,2,128,128]{3,2,1,0:T(8,128)(2,1)}, bf16[4,2,128,128]{3,2,1,0:T(8,128)(2,1)}, bf16[4,2,128,128]{3,2,1,0:T(8,128)(2,1)}, bf16[4,2,128,128]{3,2,1,0:T(8,128)(2,1)}) custom-call(s32[2]{0:T(128)} %pad_add_fusion.scalars_ref, bf16[4,2,128,128]{3,2,1,0:T(8,128)(2,1)} %get-tuple-element.18.refs_0_, bf16[4,2,128,128]{3,2,1,0:T(8,128)(2,1)} %copy-done.7, ...), custom_call_target="tpu_custom_call" | custom-call | bytes 2097152 | tf_op jit(solution)/shard_map/pallas_call | solution.py:213
  42.8 1.0 collective-permute-start.5
  43.7 2.1 %collective-permute-start.6 = (bf16[4,2,128,128]{3,2,1,0:T(8,128)(2,1)}, bf16[4,2,128,128]{3,2,1,0:T(8,128)(2,1)S(1)}, u32[]{:S(2)}, u32[]{:S(2)}) collective-permute-start(bf16[4,2,128,128]{3,2,1,0:T(8,128)(2,1)} %get-tuple-element.24), channel_id=1, source_target_pairs={{0,8},{1,9},{2,10},{3,11},{4,12},{5,13},{6,14},{7,15},{8,0},{9,1},... | collective-permute-start | bytes 786440 | tf_op jit(solution)/shard_map/ppermute | solution.py:252
  45.9 1.4 %collective-permute-start.7 = (bf16[4,2,128,128]{3,2,1,0:T(8,128)(2,1)}, bf16[4,2,128,128]{3,2,1,0:T(8,128)(2,1)S(1)}, u32[]{:S(2)}, u32[]{:S(2)}) collective-permute-start(bf16[4,2,128,128]{3,2,1,0:T(8,128)(2,1)} %get-tuple-element.25), channel_id=1, source_target_pairs={{0,12},{1,13},{2,14},{3,15},{4,8},{5,9},{6,10},{7,11},{8,4},{9,5},... | collective-permute-start | bytes 786440 | tf_op jit(solution)/shard_map/ppermute | solution.py:252
  47.3 0.7 copy-done.16
  47.9 0.6 dynamic_slice.33
  48.5 0.0 copy-done.17
  48.6 0.6 dynamic_slice.32
  49.2 1.9 %stack.42.refs_0_ = s32[8]{0:T(128)} concatenate(s32[1]{0:T(128)} %dynamic_slice.32, s32[1]{0:T(128)} %dynamic_slice.33, s32[1]{0:T(128)} %bitcast, s32[1]{0:T(128)} %bitcast.1, s32[1]{0:T(128)} %bitcast.4, s32[1]{0:T(128)} %bitcast.5, s32[1]{0:T(128)} %bitcast.6, s32[1]{0:T(128)} %bitcast.7), dimensions={0} | concatenate | bytes 64 | tf_op jit(solution)/shard_map/stack | solution.py:306
  51.1 0.0 collective-permute-done.refs_4_.refs_6_
  51.1 0.0 collective-permute-done.1.refs_6_.refs_8_
  51.1 3.3 %collective-permute-done.5.refs_2_ = bf16[4,2,128,128]{3,2,1,0:T(8,128)(2,1)S(1)} collective-permute-done((bf16[4,2,128,128]{3,2,1,0:T(8,128)(2,1)}, bf16[4,2,128,128]{3,2,1,0:T(8,128)(2,1)S(1)}, u32[]{:S(2)}, u32[]{:S(2)}) %collective-permute-start.5) | collective-permute-done | bytes 262176 | tf_op jit(solution)/shard_map/ppermute | solution.py:252
  54.4 10.6 %collective-permute-done.6.refs_3_ = bf16[4,2,128,128]{3,2,1,0:T(8,128)(2,1)S(1)} collective-permute-done((bf16[4,2,128,128]{3,2,1,0:T(8,128)(2,1)}, bf16[4,2,128,128]{3,2,1,0:T(8,128)(2,1)S(1)}, u32[]{:S(2)}, u32[]{:S(2)}) %collective-permute-start.6) | collective-permute-done | bytes 262176 | tf_op jit(solution)/shard_map/ppermute | solution.py:252
  65.1 0.0 collective-permute-done.7.refs_4_
  65.1 0.0 copy-done.12
  65.1 0.7 copy-done.14
  65.8 0.1 copy-done.15
  65.9 13.3 %shard_map.89 = (bf16[16,128,128]{2,1,0:T(8,128)(2,1)}, bf16[2048,128]{1,0:T(8,128)(2,1)}, bf16[2048,128]{1,0:T(8,128)(2,1)}) custom-call(s32[8]{0:T(128)} %stack.42.refs_0_, bf16[4,2,128,128]{3,2,1,0:T(8,128)(2,1)} %get-tuple-element.22.refs_1_, bf16[4,2,128,128]{3,2,1,0:T(8,128)(2,1)} %copy-done.13, bf16[4,2,128,128]{3,2,1,0:T(8,128)(2,1)} %copy-done.14, ...), custom_call_target="tpu_custom_call" | custom-call | flops 3397386240 | bytes 3670016 | tf_op jit(solution)/shard_map/pallas_call | solution.py:162
  79.1 0.0 all-to-all-done.refs_1_.refs_2_
  79.1 0.0 copy-start.2
  79.2 7.7 %all-to-all-start.2 = ((bf16[16,128,128]{2,1,0:T(8,128)(2,1)}), bf16[16,128,128]{2,1,0:T(8,128)(2,1)S(1)}, u32[]{:S(2)}, u32[]{:S(2)}) async-start(bf16[16,128,128]{2,1,0:T(8,128)(2,1)} %get-tuple-element.26), calls=%async_computation.2 | async-start | bytes 1048576 | tf_op jit(solution)/shard_map/all_to_all | solution.py:310
  86.9 0.0 copy-start.3
  86.9 0.1 collective-permute-start.11
  87.0 2.0 %stack.37.refs_0_ = s32[5]{0:T(128)} concatenate(s32[1]{0:T(128)} %dynamic_slice.32, s32[1]{0:T(128)} %dynamic_slice.33, s32[1]{0:T(128)} %bitcast, s32[1]{0:T(128)} %bitcast.1, s32[1]{0:T(128)} %constant.33.clone.1.scalars_ref), dimensions={0} | concatenate | bytes 40 | tf_op jit(solution)/shard_map/stack | solution.py:306
  89.0 0.5 collective-permute-start.9
  89.5 0.0 collective-permute-done.11
  89.5 1.0 add_convert_fusion
  90.5 13.0 %shard_map.86 = (bf16[16,128,128]{2,1,0:T(8,128)(2,1)}, bf16[2048,128]{1,0:T(8,128)(2,1)}, bf16[2048,128]{1,0:T(8,128)(2,1)}) custom-call(s32[5]{0:T(128)} %stack.37.refs_0_, bf16[16,2,128,128]{3,2,1,0:T(8,128)(2,1)} %copy-done.2, bf16[16,2,128,128]{3,2,1,0:T(8,128)(2,1)} %copy-done.2, bf16[1024,256]{1,0:T(8,128)(2,1)} %refs_5_.3, ...), custom_call_target="tpu_custom_call" | custom-call | flops 3397386240 | bytes 3670016 | tf_op jit(solution)/shard_map/pallas_call | solution.py:162
  103.6 1.0 constant_dynamic-slice_fusion.1
  104.5 0.1 collective-permute-start.10
  104.6 0.0 all-to-all-done.2.refs_1_
  104.6 0.8 copy-done
  105.4 6.9 %all-to-all-start.1 = ((bf16[16,128,128]{2,1,0:T(8,128)(2,1)}), bf16[16,128,128]{2,1,0:T(8,128)(2,1)S(1)}, u32[]{:S(2)}, u32[]{:S(2)}) async-start(bf16[16,128,128]{2,1,0:T(8,128)(2,1)} %get-tuple-element.17), calls=%async_computation.1 | async-start | bytes 1048576 | tf_op jit(solution)/shard_map/all_to_all | solution.py:310
  112.3 0.0 copy-start.4
  112.4 0.0 copy-start.6
  112.4 0.0 collective-permute-done.9
  112.4 0.1 add_convert_fusion.2
  112.5 0.9 copy-done.4
  113.4 0.2 collective-permute-start.8
  113.6 0.0 collective-permute-done.10
  113.7 0.1 add_convert_fusion.1
  113.7 0.9 pad_maximum_fusion.1
  114.6 0.4 collective-permute-done.8
  115.0 0.1 add_convert_fusion.3
  115.1 0.9 pad_maximum_fusion
  115.9 11.9 %all-to-all-done.1.refs_0_ = bf16[16,128,128]{2,1,0:T(8,128)(2,1)S(1)} async-done(((bf16[16,128,128]{2,1,0:T(8,128)(2,1)}), bf16[16,128,128]{2,1,0:T(8,128)(2,1)S(1)}, u32[]{:S(2)}, u32[]{:S(2)}) %all-to-all-start.1) | async-done | bytes 524320 | tf_op jit(solution)/shard_map/all_to_all | solution.py:310
  127.8 0.8 copy-done.1
  128.6 2.4 %shard_map.90 = bf16[128,4096]{1,0:T(8,128)(2,1)} custom-call(s32[1]{0:T(128)} %constant.33.clone.1.scalars_ref, bf16[16,128,128]{2,1,0:T(8,128)(2,1)} %copy-done.1, bf16[16,128,128]{2,1,0:T(8,128)(2,1)} %copy-done), custom_call_target="tpu_custom_call" | custom-call | bytes 2097152 | tf_op jit(solution)/shard_map/pallas_call | solution.py:213
  (23 shorter events, 0.1 us)
Async XLA Ops:
  3.1 76.1 %all-to-all-start = ((bf16[16,2,128,128]{3,2,1,0:T(8,128)(2,1)}), bf16[16,2,128,128]{3,2,1,0:T(8,128)(2,1)S(1)}, u32[]{:S(2)}, u32[]{:S(2)}) async-start(bf16[16,2,128,128]{3,2,1,0:T(8,128)(2,1)} %shard_map.85), calls=%async_computation | async-start | bytes 2097152 | tf_op jit(solution)/shard_map/all_to_all | solution.py:259
  12.1 6.8 %copy-start.10 = (bf16[1024,256]{1,0:T(8,128)(2,1)S(1)}, bf16[1024,256]{1,0:T(8,128)(2,1)}, u32[]{:S(2)}) copy-start(bf16[1024,256]{1,0:T(8,128)(2,1)} %refs_5_.3) | copy-start | bytes 1572868
  12.1 6.8 %copy-start.11 = (bf16[1024,256]{1,0:T(8,128)(2,1)S(1)}, bf16[1024,256]{1,0:T(8,128)(2,1)}, u32[]{:S(2)}) copy-start(bf16[1024,256]{1,0:T(8,128)(2,1)} %refs_7_.1) | copy-start | bytes 1572868
  15.3 15.1 %collective-permute-start.2 = (bf16[4,2,128,128]{3,2,1,0:T(8,128)(2,1)}, bf16[4,2,128,128]{3,2,1,0:T(8,128)(2,1)S(1)}, u32[]{:S(2)}, u32[]{:S(2)}) collective-permute-start(bf16[4,2,128,128]{3,2,1,0:T(8,128)(2,1)} %get-tuple-element.19), channel_id=1, source_target_pairs={{0,1},{1,0},{2,3},{3,2},{4,5},{5,4},{6,7},{7,6},{8,9},{9,8},{10,11... | collective-permute-start | bytes 786440 | tf_op jit(solution)/shard_map/ppermute | solution.py:252
  17.3 14.5 %collective-permute-start.3 = (bf16[4,2,128,128]{3,2,1,0:T(8,128)(2,1)}, bf16[4,2,128,128]{3,2,1,0:T(8,128)(2,1)S(1)}, u32[]{:S(2)}, u32[]{:S(2)}) collective-permute-start(bf16[4,2,128,128]{3,2,1,0:T(8,128)(2,1)} %get-tuple-element.20), channel_id=1, source_target_pairs={{0,2},{1,3},{2,0},{3,1},{4,6},{5,7},{6,4},{7,5},{8,10},{9,11},{10,... | collective-permute-start | bytes 786440 | tf_op jit(solution)/shard_map/ppermute | solution.py:252
  18.7 20.3 %collective-permute-start.4 = (bf16[4,2,128,128]{3,2,1,0:T(8,128)(2,1)}, bf16[4,2,128,128]{3,2,1,0:T(8,128)(2,1)S(1)}, u32[]{:S(2)}, u32[]{:S(2)}) collective-permute-start(bf16[4,2,128,128]{3,2,1,0:T(8,128)(2,1)} %get-tuple-element.21), channel_id=1, source_target_pairs={{0,3},{1,2},{2,1},{3,0},{4,7},{5,6},{6,5},{7,4},{8,11},{9,10},{10,... | collective-permute-start | bytes 786440 | tf_op jit(solution)/shard_map/ppermute | solution.py:252
  18.9 32.2 %collective-permute-start = (bf16[1024,256]{1,0:T(8,128)(2,1)S(1)}, bf16[1024,256]{1,0:T(8,128)(2,1)S(1)}, u32[]{:S(2)}, u32[]{:S(2)}) collective-permute-start(bf16[1024,256]{1,0:T(8,128)(2,1)S(1)} %copy-done.10), channel_id=1, source_target_pairs={{0,16},{16,0},{1,17},{17,1},{2,18},{18,2},{3,19},{19,3},{4,20},{20... | collective-permute-start | bytes 1572872 | tf_op jit(solution)/shard_map/ppermute | solution.py:285
  18.9 32.2 %collective-permute-start.1 = (bf16[1024,256]{1,0:T(8,128)(2,1)S(1)}, bf16[1024,256]{1,0:T(8,128)(2,1)}, u32[]{:S(2)}, u32[]{:S(2)}) collective-permute-start(bf16[1024,256]{1,0:T(8,128)(2,1)S(1)} %copy-done.11), channel_id=1, source_target_pairs={{0,16},{16,0},{1,17},{17,1},{2,18},{18,2},{3,19},{19,3},{4,20},{20... | collective-permute-start | bytes 1572872 | tf_op jit(solution)/shard_map/ppermute | solution.py:286
  30.4 8.7 %copy-start.7 = (bf16[4,2,128,128]{3,2,1,0:T(8,128)(2,1)}, bf16[4,2,128,128]{3,2,1,0:T(8,128)(2,1)S(1)}, u32[]{:S(2)}) copy-start(bf16[4,2,128,128]{3,2,1,0:T(8,128)(2,1)S(1)} %collective-permute-done.2.refs_1_) | copy-start | bytes 786436
  31.7 7.3 %copy-start.8 = (bf16[4,2,128,128]{3,2,1,0:T(8,128)(2,1)}, bf16[4,2,128,128]{3,2,1,0:T(8,128)(2,1)S(1)}, u32[]{:S(2)}) copy-start(bf16[4,2,128,128]{3,2,1,0:T(8,128)(2,1)S(1)} %collective-permute-done.3.refs_2_) | copy-start | bytes 786436
  39.0 0.7 copy-start.9
  42.8 11.7 %collective-permute-start.5 = (bf16[4,2,128,128]{3,2,1,0:T(8,128)(2,1)}, bf16[4,2,128,128]{3,2,1,0:T(8,128)(2,1)S(1)}, u32[]{:S(2)}, u32[]{:S(2)}) collective-permute-start(bf16[4,2,128,128]{3,2,1,0:T(8,128)(2,1)} %get-tuple-element.23), channel_id=1, source_target_pairs={{0,4},{1,5},{2,6},{3,7},{4,0},{5,1},{6,2},{7,3},{8,12},{9,13},{10,... | collective-permute-start | bytes 786440 | tf_op jit(solution)/shard_map/ppermute | solution.py:252
  43.7 21.3 %collective-permute-start.6 = (bf16[4,2,128,128]{3,2,1,0:T(8,128)(2,1)}, bf16[4,2,128,128]{3,2,1,0:T(8,128)(2,1)S(1)}, u32[]{:S(2)}, u32[]{:S(2)}) collective-permute-start(bf16[4,2,128,128]{3,2,1,0:T(8,128)(2,1)} %get-tuple-element.24), channel_id=1, source_target_pairs={{0,8},{1,9},{2,10},{3,11},{4,12},{5,13},{6,14},{7,15},{8,0},{9,1},... | collective-permute-start | bytes 786440 | tf_op jit(solution)/shard_map/ppermute | solution.py:252
  45.9 19.2 %collective-permute-start.7 = (bf16[4,2,128,128]{3,2,1,0:T(8,128)(2,1)}, bf16[4,2,128,128]{3,2,1,0:T(8,128)(2,1)S(1)}, u32[]{:S(2)}, u32[]{:S(2)}) collective-permute-start(bf16[4,2,128,128]{3,2,1,0:T(8,128)(2,1)} %get-tuple-element.25), channel_id=1, source_target_pairs={{0,12},{1,13},{2,14},{3,15},{4,8},{5,9},{6,10},{7,11},{8,4},{9,5},... | collective-permute-start | bytes 786440 | tf_op jit(solution)/shard_map/ppermute | solution.py:252
  47.3 0.7 copy-start.16
  47.9 0.7 copy-start.17
  51.1 14.0 %copy-start.12 = (bf16[1024,256]{1,0:T(8,128)(2,1)}, bf16[1024,256]{1,0:T(8,128)(2,1)S(1)}, u32[]{:S(2)}) copy-start(bf16[1024,256]{1,0:T(8,128)(2,1)S(1)} %collective-permute-done.refs_4_.refs_6_) | copy-start | bytes 1572868
  54.4 10.6 %copy-start.13 = (bf16[4,2,128,128]{3,2,1,0:T(8,128)(2,1)}, bf16[4,2,128,128]{3,2,1,0:T(8,128)(2,1)S(1)}, u32[]{:S(2)}) copy-start(bf16[4,2,128,128]{3,2,1,0:T(8,128)(2,1)S(1)} %collective-permute-done.5.refs_2_) | copy-start | bytes 786436
  65.1 0.7 copy-start.14
  65.1 0.8 copy-start.15
  79.1 9.8 %copy-start.2 = (bf16[16,2,128,128]{3,2,1,0:T(8,128)(2,1)}, bf16[16,2,128,128]{3,2,1,0:T(8,128)(2,1)S(1)}, u32[]{:S(2)}) copy-start(bf16[16,2,128,128]{3,2,1,0:T(8,128)(2,1)S(1)} %all-to-all-done.refs_1_.refs_2_) | copy-start | bytes 3145732
  79.2 7.7 %copy-start.5 = (bf16[2048,128]{1,0:T(8,128)(2,1)S(1)}, bf16[2048,128]{1,0:T(8,128)(2,1)}, u32[]{:S(2)}) copy-start(bf16[2048,128]{1,0:T(8,128)(2,1)} %get-tuple-element.30) | copy-start | bytes 1572868
  79.2 25.5 %all-to-all-start.2 = ((bf16[16,128,128]{2,1,0:T(8,128)(2,1)}), bf16[16,128,128]{2,1,0:T(8,128)(2,1)S(1)}, u32[]{:S(2)}, u32[]{:S(2)}) async-start(bf16[16,128,128]{2,1,0:T(8,128)(2,1)} %get-tuple-element.26), calls=%async_computation.2 | async-start | bytes 1048576 | tf_op jit(solution)/shard_map/all_to_all | solution.py:310
  86.9 2.1 %copy-start.3 = (bf16[2048,128]{1,0:T(8,128)(2,1)S(1)}, bf16[2048,128]{1,0:T(8,128)(2,1)}, u32[]{:S(2)}) copy-start(bf16[2048,128]{1,0:T(8,128)(2,1)} %get-tuple-element.28) | copy-start | bytes 1572868
  86.9 2.6 %collective-permute-start.11 = (bf16[1024,128]{1,0:T(8,128)(2,1)S(1)}, bf16[1024,128]{1,0:T(8,128)(2,1)}, u32[]{:S(2)}, u32[]{:S(2)}) collective-permute-start(bf16[1024,128]{1,0:T(8,128)(2,1)S(1)} %constant_dynamic-slice_fusion), channel_id=1, source_target_pairs={{0,16},{16,0},{1,17},{17,1},{2,18},{18,2},{3,19},{19,3},{4,20},{20... | collective-permute-start | bytes 786440 | tf_op jit(solution)/shard_map/ppermute | solution.py:292
  89.0 23.4 %collective-permute-start.9 = (bf16[1024,128]{1,0:T(8,128)(2,1)S(1)}, bf16[1024,128]{1,0:T(8,128)(2,1)S(1)}, u32[]{:S(2)}, u32[]{:S(2)}) collective-permute-start(bf16[1024,128]{1,0:T(8,128)(2,1)S(1)} %constant_dynamic-slice_fusion.2), channel_id=1, source_target_pairs={{0,16},{16,0},{1,17},{17,1},{2,18},{18,2},{3,19},{19,3},{4,20},{20... | collective-permute-start | bytes 786440 | tf_op jit(solution)/shard_map/ppermute | solution.py:292
  104.5 9.1 %collective-permute-start.10 = (bf16[1024,128]{1,0:T(8,128)(2,1)S(1)}, bf16[1024,128]{1,0:T(8,128)(2,1)S(1)}, u32[]{:S(2)}, u32[]{:S(2)}) collective-permute-start(bf16[1024,128]{1,0:T(8,128)(2,1)S(1)} %constant_dynamic-slice_fusion.1), channel_id=1, source_target_pairs={{0,16},{16,0},{1,17},{17,1},{2,18},{18,2},{3,19},{19,3},{4,20},{20... | collective-permute-start | bytes 786440 | tf_op jit(solution)/shard_map/ppermute | solution.py:292
  104.6 0.8 copy-start
  105.4 22.4 %all-to-all-start.1 = ((bf16[16,128,128]{2,1,0:T(8,128)(2,1)}), bf16[16,128,128]{2,1,0:T(8,128)(2,1)S(1)}, u32[]{:S(2)}, u32[]{:S(2)}) async-start(bf16[16,128,128]{2,1,0:T(8,128)(2,1)} %get-tuple-element.17), calls=%async_computation.1 | async-start | bytes 1048576 | tf_op jit(solution)/shard_map/all_to_all | solution.py:310
  112.3 1.0 copy-start.4
  112.4 1.3 copy-start.6
  113.4 1.6 %collective-permute-start.8 = (bf16[1024,128]{1,0:T(8,128)(2,1)S(1)}, bf16[1024,128]{1,0:T(8,128)(2,1)S(1)}, u32[]{:S(2)}, u32[]{:S(2)}) collective-permute-start(bf16[1024,128]{1,0:T(8,128)(2,1)S(1)} %constant_dynamic-slice_fusion.3), channel_id=1, source_target_pairs={{0,16},{16,0},{1,17},{17,1},{2,18},{18,2},{3,19},{19,3},{4,20},{20... | collective-permute-start | bytes 786440 | tf_op jit(solution)/shard_map/ppermute | solution.py:292
  127.8 0.8 copy-start.1
